TPU v7x, 32 devices: a whole 2x2x4 slice. The times are simulated.
32 devices in a mesh: slab: 4 (over y, x), member: 8 (over z, core).
Axes of the slice: x: 2, y: 2, z: 4, core: 2. Of those that a mesh axis runs over, the one named last changes fastest.
Arguments:
- prior_sample_group: float32 [64, 64, 3, 512], P('member', 'slab'), may hold values from -6 to 6
- obs_values: float32 [4, 256], replicated, may hold values from -6 to 6
- obs_variance: float32 [4, 256], replicated, may hold values from 0.25 to 4
- obs_perturb: float32 [4, 256, 64], replicated, may hold values from -6 to 6
- obs_offset: int32 [4, 256], replicated, may hold values from 0 to 8191
- owner_order: int32 [4], replicated, may hold values from 0 to 3, each once
- taper_cutoff: int32 [4, 256], replicated, may hold values from 32 to 64
Outputs:
- analysis: float32 [64, 98304], P(None, ('slab', 'member'))
Inputs may be any that keep to these rules, and one draw needn't show every extreme that they name: A permutation of the slab indices; batch b belongs to slab owner_order[b mod the number of slabs]. `obs_offset`: row-major offset within the owner slab's block of 16 x 512 cells.
All inputs are finite; a program needn't handle non-finite values.
Results may differ from a plain program's by a relative error of at most 0.0003.
Values sent between devices are 32-bit elements; how exact they have to be, the bound alone decides.
No kernel may reach another device: no remote copies, remote signals or barrier semaphores. Data moves between devices by JAX's collectives and lax.ppermute only.
A program may use at most 64 MiB of HBM per device.

v0:
```python
import jax
import jax.numpy as jnp
from jax import lax
from jax.sharding import PartitionSpec as P

NBATCH = 4


courant = 0.3
rotation = 0.1


def padded(block, sides, width):
    for axis, dim in sides:
        count = lax.axis_size(axis)
        forward = [(i, i + 1) for i in range(count - 1)]
        forward.append((count - 1, 0))
        backward = [(target, source) for source, target in forward]
        low = lax.ppermute(
            lax.slice_in_dim(block, block.shape[dim] - width, None, axis=dim), axis, forward
        )
        high = lax.ppermute(lax.slice_in_dim(block, 0, width, axis=dim), axis, backward)
        block = jnp.concatenate([low, block, high], axis=dim)
    return block


def spread_2(shard, axis, root):
    mine = lax.axis_index(axis) == root
    return lax.psum(jnp.where(mine, shard, jnp.zeros_like(shard)), axis)


def centred_y(sample):
    return (jnp.roll(sample, -1, axis=2) - jnp.roll(sample, 1, axis=2)) * 0.5


def fluid_layer_timestep(extended):
    height = extended[:, :, 0]
    velocity_x = extended[:, :, 1]
    velocity_y = extended[:, :, 2]
    spread = (velocity_x[:, 2:] - velocity_x[:, :-2]) * 0.5 + centred_y(velocity_y)[:, 1:-1]
    new_height = height[:, 1:-1] - courant * spread
    slope_x = (new_height[:, 2:] - new_height[:, :-2]) * 0.5
    slope_y = centred_y(new_height)[:, 1:-1]
    new_x = velocity_x[:, 2:-2] - courant * slope_x + rotation * velocity_y[:, 2:-2]
    new_y = velocity_y[:, 2:-2] - courant * slope_y - rotation * velocity_x[:, 2:-2]
    return jnp.stack([new_height[:, 1:-1], new_x, new_y], axis=2)


def observe_layout(offsets, owner_slab, cells_x, cells_y):
    cell_index = owner_slab * (cells_x * cells_y) + offsets
    obs_row = cell_index // cells_y
    column = cell_index % cells_y
    return (obs_row, column, obs_row * (3 * cells_y) + column)


def taper_weights(var_index, obs_row, obs_column, cutoff, total_x, cells_y):
    var_row = var_index // (3 * cells_y)
    var_column = var_index % cells_y
    gap_x = jnp.abs(var_row[:, None] - obs_row[None, :])
    gap_x = jnp.minimum(gap_x, total_x - gap_x)
    gap_y = jnp.abs(var_column[:, None] - obs_column[None, :])
    gap_y = jnp.minimum(gap_y, cells_y - gap_y)
    distance = jnp.sqrt((gap_x * gap_x + gap_y * gap_y).astype(jnp.float32))
    return jnp.square(jnp.maximum(0.0, 1.0 - distance / cutoff.astype(jnp.float32)[None, :]))


def solve_batch(observed, values_in, variance, perturb):
    members = observed.shape[1]
    spread = observed - jnp.mean(observed, axis=1, keepdims=True)
    system = jnp.dot(spread, spread.T, precision=lax.Precision.HIGHEST) / (members - 1) + jnp.diag(
        variance
    )
    target = values_in[:, None] + jnp.sqrt(variance)[:, None] * perturb - observed
    factor = jnp.linalg.cholesky(system)
    forward = lax.linalg.triangular_solve(factor, target, left_side=True, lower=True)
    weights = lax.linalg.triangular_solve(
        factor, forward, left_side=True, lower=True, transpose_a=True
    )
    return (spread, weights)


def apply_batch(system_quantities, spread, weights, taper_rho):
    members = system_quantities.shape[0]
    anomaly = system_quantities - jnp.mean(system_quantities, axis=0, keepdims=True)
    covariance = lax.dot_general(
        anomaly, spread, (((0,), (1,)), ((), ())), precision=lax.Precision.HIGHEST
    ) / (members - 1)
    local_gain = covariance * taper_rho
    return system_quantities + lax.dot_general(
        weights, local_gain, (((0,), (1,)), ((), ())), precision=lax.Precision.HIGHEST
    )


def on_device(
    prior_sample_group, obs_values, obs_variance, obs_perturb, obs_offset, owner_order, taper_cutoff
):
    slab_count = lax.axis_size("slab")
    shards = lax.axis_size("member")
    cells_x = prior_sample_group.shape[1]
    cells_y = prior_sample_group.shape[3]
    total_x = cells_x * slab_count
    bordered_grid = padded(prior_sample_group, (("slab", 1),), 4)
    predict_ahead = fluid_layer_timestep(fluid_layer_timestep(bordered_grid))
    unrolled_array = predict_ahead.reshape(predict_ahead.shape[0], -1)
    system_quantities = lax.all_to_all(
        unrolled_array, "member", split_axis=1, concat_axis=0, tiled=True
    )
    var_count = system_quantities.shape[1]
    first_var = (lax.axis_index("slab") * shards + lax.axis_index("member")) * var_count
    var_index = first_var + lax.iota(jnp.int32, var_count)
    for batch_no in range(NBATCH):
        owner_slab = owner_order[batch_no % slab_count]
        obs_row, obs_column, obs_flat = observe_layout(
            obs_offset[batch_no], owner_slab, cells_x, cells_y
        )
        selector = (obs_flat[:, None] == var_index[None, :]).astype(jnp.float32)
        partial_obs = lax.dot_general(
            selector, system_quantities, (((1,), (1,)), ((), ())), precision=lax.Precision.HIGHEST
        )
        observed = lax.psum(partial_obs, "member")
        spread, weights = solve_batch(
            observed, obs_values[batch_no], obs_variance[batch_no], obs_perturb[batch_no]
        )
        stacked = spread_2(jnp.stack([spread, weights]), "slab", owner_slab)
        spread = stacked[0]
        weights = stacked[1]
        taper_rho = taper_weights(
            var_index, obs_row, obs_column, taper_cutoff[batch_no], total_x, cells_y
        )
        system_quantities = apply_batch(system_quantities, spread, weights, taper_rho)
    return system_quantities


def solution(mesh):
    in_specs = (P("member", "slab", None, None), P(), P(), P(), P(), P(), P())
    out_specs = P(None, ("slab", "member"))
    return jax.shard_map(
        on_device, mesh=mesh, in_specs=in_specs, out_specs=out_specs, check_vma=False
    )
```

profile of v0, /device:TPU:0, one launch (start us, length us, event | category | flops | bytes accessed | tf_op | source)
XLA Modules:
  0.0 754.6 jit_solution(17040334949533999156)
XLA Ops:
  6.5 1.2 fusion.172
  7.7 3.0 collective-permute-start
  10.7 1.0 collective-permute-start.1
  11.8 1.5 fusion.183
  17.5 3.6 collective-permute-done.1
  21.1 1.3 pad_maximum_fusion
  26.2 1.3 copy.46
  27.5 4.9 all-to-all-start
  32.6 20.8 %all-to-all-done = f32[8,8,3072]{2,0,1:T(8,128)S(1)} async-done(((f32[8,8,3072]{2,0,1:T(8,128)}), f32[8,8,3072]{2,0,1:T(8,128)S(1)}, u32[]{:S(2)}, u32[]{:S(2)}) %all-to-all-start) | async-done | bytes 786464 | tf_op jit(solution)/shard_map/all_to_all | solution.py:105
  53.4 2.3 fusion.46
  56.7 51.9 %all-reduce.10.cloned.1.call-done = f32[256,64]{0,1:T(8,128)} async-done(((f32[256,64]{0,1:T(8,128)}), f32[256,64]{0,1:T(8,128)}) %all-reduce.10.cloned.1.call-update) | async-done | bytes 65552 | tf_op jit(solution)/shard_map/psum | solution.py:120
  109.5 1.3 fusion.59
  111.1 11.7 %cholesky.214 = f32[128,128]{1,0:T(8,128)S(1)} custom-call(f32[128,128]{1,0:T(8,128)S(1)} %cholesky.346), custom_call_target="Cholesky" | custom-call | tf_op jit(solution)/shard_map/jit(cholesky)/cholesky | solution.py:74
  122.8 9.8 %custom-call.23 = f32[1,128,128]{1,2,0:T(8,128)S(1)} custom-call(f32[1,128,128]{2,1,0:T(8,128)S(1)} %get-tuple-element.169), custom_call_target="InvertDiagBlocksLowerTriangular" | custom-call | tf_op jit(solution)/shard_map/jit(cholesky)/cholesky | solution.py:74
  133.1 11.7 %cholesky.231 = f32[128,128]{1,0:T(8,128)S(1)} custom-call(f32[128,128]{1,0:T(8,128)S(1)} %convolution_subtract_fusion.3), custom_call_target="Cholesky" | custom-call | tf_op jit(solution)/shard_map/jit(cholesky)/cholesky | solution.py:74
  146.9 4.4 while.16
  147.9 1.4 bitcast_dynamic-update-slice_fusion.8
  149.9 1.4 bitcast_dynamic-update-slice_fusion.8
  151.3 19.7 %custom-call.25 = f32[2,128,128]{1,2,0:T(8,128)S(1)} custom-call(f32[2,128,128]{2,1,0:T(8,128)S(1)} %get-tuple-element.61), custom_call_target="InvertDiagBlocksLowerTriangular" | custom-call | tf_op jit(solution)/shard_map/triangular_solve/custom-call.4 | solution.py:76
  173.1 41.4 %all-reduce.12.cloned.1.call-done = f32[2,256,64]{1,2,0:T(8,128)} async-done(((f32[2,256,64]{1,2,0:T(8,128)}), f32[2,256,64]{1,2,0:T(8,128)}) %all-reduce.12.cloned.1.call-update) | async-done | bytes 131088 | tf_op jit(solution)/shard_map/psum | solution.py:29
  214.5 7.2 fusion.3
  221.7 3.1 fusion.184
  224.9 2.4 fusion.44
  228.1 54.0 %all-reduce.14.cloned.1.call-done = f32[256,64]{0,1:T(8,128)} async-done(((f32[256,64]{0,1:T(8,128)}), f32[256,64]{0,1:T(8,128)}) %all-reduce.14.cloned.1.call-update) | async-done | bytes 65552 | tf_op jit(solution)/shard_map/psum | solution.py:120
  282.1 0.9 reduce_sum.74
  283.0 1.3 fusion.58
  284.6 11.7 %cholesky.248 = f32[128,128]{1,0:T(8,128)S(1)} custom-call(f32[128,128]{1,0:T(8,128)S(1)} %cholesky.349), custom_call_target="Cholesky" | custom-call | tf_op jit(solution)/shard_map/jit(cholesky)/cholesky | solution.py:74
  296.3 9.8 %custom-call.26 = f32[1,128,128]{1,2,0:T(8,128)S(1)} custom-call(f32[1,128,128]{2,1,0:T(8,128)S(1)} %get-tuple-element.163), custom_call_target="InvertDiagBlocksLowerTriangular" | custom-call | tf_op jit(solution)/shard_map/jit(cholesky)/cholesky | solution.py:74
  306.6 11.7 %cholesky.265 = f32[128,128]{1,0:T(8,128)S(1)} custom-call(f32[128,128]{1,0:T(8,128)S(1)} %convolution_subtract_fusion.2), custom_call_target="Cholesky" | custom-call | tf_op jit(solution)/shard_map/jit(cholesky)/cholesky | solution.py:74
  321.0 4.2 while.17
  321.8 1.4 bitcast_dynamic-update-slice_fusion.9
  323.8 1.4 bitcast_dynamic-update-slice_fusion.9
  325.2 19.7 %custom-call.28 = f32[2,128,128]{1,2,0:T(8,128)S(1)} custom-call(f32[2,128,128]{2,1,0:T(8,128)S(1)} %get-tuple-element.63), custom_call_target="InvertDiagBlocksLowerTriangular" | custom-call | tf_op jit(solution)/shard_map/triangular_solve/custom-call.4 | solution.py:76
  347.0 41.4 %all-reduce.16.cloned.1.call-done = f32[2,256,64]{1,2,0:T(8,128)} async-done(((f32[2,256,64]{1,2,0:T(8,128)}), f32[2,256,64]{1,2,0:T(8,128)}) %all-reduce.16.cloned.1.call-update) | async-done | bytes 131088 | tf_op jit(solution)/shard_map/psum | solution.py:29
  388.3 7.2 fusion.2
  395.6 3.1 fusion.185
  398.7 2.4 fusion.42
  402.3 53.7 %all-reduce.18.cloned.1.call-done = f32[256,64]{0,1:T(8,128)} async-done(((f32[256,64]{0,1:T(8,128)}), f32[256,64]{0,1:T(8,128)}) %all-reduce.18.cloned.1.call-update) | async-done | bytes 65552 | tf_op jit(solution)/shard_map/psum | solution.py:120
  455.9 0.9 reduce_sum.76
  456.9 1.3 fusion.57
  458.4 11.7 %cholesky.282 = f32[128,128]{1,0:T(8,128)S(1)} custom-call(f32[128,128]{1,0:T(8,128)S(1)} %cholesky.352), custom_call_target="Cholesky" | custom-call | tf_op jit(solution)/shard_map/jit(cholesky)/cholesky | solution.py:74
  470.2 9.8 %custom-call.29 = f32[1,128,128]{1,2,0:T(8,128)S(1)} custom-call(f32[1,128,128]{2,1,0:T(8,128)S(1)} %get-tuple-element.157), custom_call_target="InvertDiagBlocksLowerTriangular" | custom-call | tf_op jit(solution)/shard_map/jit(cholesky)/cholesky | solution.py:74
  480.5 11.7 %cholesky.299 = f32[128,128]{1,0:T(8,128)S(1)} custom-call(f32[128,128]{1,0:T(8,128)S(1)} %convolution_subtract_fusion.1), custom_call_target="Cholesky" | custom-call | tf_op jit(solution)/shard_map/jit(cholesky)/cholesky | solution.py:74
  494.8 4.1 while.18
  495.6 1.4 bitcast_dynamic-update-slice_fusion.10
  497.6 1.4 bitcast_dynamic-update-slice_fusion.10
  499.0 19.7 %custom-call.31 = f32[2,128,128]{1,2,0:T(8,128)S(1)} custom-call(f32[2,128,128]{2,1,0:T(8,128)S(1)} %get-tuple-element.65), custom_call_target="InvertDiagBlocksLowerTriangular" | custom-call | tf_op jit(solution)/shard_map/triangular_solve/custom-call.4 | solution.py:76
  520.8 41.4 %all-reduce.20.cloned.1.call-done = f32[2,256,64]{1,2,0:T(8,128)} async-done(((f32[2,256,64]{1,2,0:T(8,128)}), f32[2,256,64]{1,2,0:T(8,128)}) %all-reduce.20.cloned.1.call-update) | async-done | bytes 131088 | tf_op jit(solution)/shard_map/psum | solution.py:29
  562.2 7.2 fusion.1
  569.4 3.1 fusion.186
  572.6 2.4 fusion.40
  575.9 53.9 %all-reduce.22.cloned.1.call-done = f32[256,64]{0,1:T(8,128)} async-done(((f32[256,64]{0,1:T(8,128)}), f32[256,64]{0,1:T(8,128)}) %all-reduce.22.cloned.1.call-update) | async-done | bytes 65552 | tf_op jit(solution)/shard_map/psum | solution.py:120
  629.8 0.9 reduce_sum.78
  630.7 1.3 fusion.56
  632.3 11.7 %cholesky.316 = f32[128,128]{1,0:T(8,128)S(1)} custom-call(f32[128,128]{1,0:T(8,128)S(1)} %cholesky.355), custom_call_target="Cholesky" | custom-call | tf_op jit(solution)/shard_map/jit(cholesky)/cholesky | solution.py:74
  644.0 9.8 %custom-call.32 = f32[1,128,128]{1,2,0:T(8,128)S(1)} custom-call(f32[1,128,128]{2,1,0:T(8,128)S(1)} %get-tuple-element.151), custom_call_target="InvertDiagBlocksLowerTriangular" | custom-call | tf_op jit(solution)/shard_map/jit(cholesky)/cholesky | solution.py:74
  654.3 11.7 %cholesky.333 = f32[128,128]{1,0:T(8,128)S(1)} custom-call(f32[128,128]{1,0:T(8,128)S(1)} %convolution_subtract_fusion), custom_call_target="Cholesky" | custom-call | tf_op jit(solution)/shard_map/jit(cholesky)/cholesky | solution.py:74
  668.7 4.2 while.19
  669.6 1.3 bitcast_dynamic-update-slice_fusion.11
  671.5 1.3 bitcast_dynamic-update-slice_fusion.11
  672.9 19.7 %custom-call.34 = f32[2,128,128]{1,2,0:T(8,128)S(1)} custom-call(f32[2,128,128]{2,1,0:T(8,128)S(1)} %get-tuple-element.67), custom_call_target="InvertDiagBlocksLowerTriangular" | custom-call | tf_op jit(solution)/shard_map/triangular_solve/custom-call.4 | solution.py:76
  694.6 41.4 %all-reduce.24.cloned.1.call-done = f32[2,256,64]{1,2,0:T(8,128)} async-done(((f32[2,256,64]{1,2,0:T(8,128)}), f32[2,256,64]{1,2,0:T(8,128)}) %all-reduce.24.cloned.1.call-update) | async-done | bytes 131088 | tf_op jit(solution)/shard_map/psum | solution.py:29
  736.0 7.2 fusion
  743.3 4.0 convolution_add_fusion
  (186 shorter events, 28.3 us)
Async XLA Ops:
  7.7 9.7 %collective-permute-start = (f32[8,4,3,512]{3,1,2,0:T(4,128)S(1)}, f32[8,4,3,512]{3,1,2,0:T(4,128)S(1)}, u32[]{:S(2)}, u32[]{:S(2)}) collective-permute-start(f32[8,4,3,512]{3,1,2,0:T(4,128)S(1)} %get-tuple-element.127), channel_id=1, source_target_pairs={{0,8},{8,16},{16,24},{24,0},{1,9},{9,17},{17,25},{25,1},{2,10},{10... | collective-permute-start | bytes 589832 | tf_op jit(solution)/shard_map/ppermute | solution.py:19
  10.7 10.3 %collective-permute-start.1 = (f32[8,4,3,512]{3,1,2,0:T(4,128)S(1)}, f32[8,4,3,512]{3,1,2,0:T(4,128)S(1)}, u32[]{:S(2)}, u32[]{:S(2)}) collective-permute-start(f32[8,4,3,512]{3,1,2,0:T(4,128)S(1)} %get-tuple-element.128), channel_id=1, source_target_pairs={{8,0},{16,8},{24,16},{0,24},{9,1},{17,9},{25,17},{1,25},{10,2},{18... | collective-permute-start | bytes 589832 | tf_op jit(solution)/shard_map/ppermute | solution.py:22
  25.0 7.5 copy-start.9
  25.0 7.5 copy-start.10
  25.0 7.5 copy-start.11
  27.5 25.8 %all-to-all-start = ((f32[8,8,3072]{2,0,1:T(8,128)}), f32[8,8,3072]{2,0,1:T(8,128)S(1)}, u32[]{:S(2)}, u32[]{:S(2)}) async-start(f32[8,8,3072]{2,0,1:T(8,128)} %copy.46), calls=%async_computation | async-start | bytes 1572864 | tf_op jit(solution)/shard_map/all_to_all | solution.py:105
  32.4 76.2 %all-reduce.10.cloned.1.call-start = ((), (), s32[]{:S(2)}) async-start(), calls=%async_computation.1 | async-start | bytes 131072 | tf_op jit(solution)/shard_map/psum | solution.py:120
  32.6 138.4 %copy-start.4 = (f32[4,256,64]{1,2,0:T(8,128)S(1)}, f32[4,256,64]{1,2,0:T(8,128)}, u32[]{:S(2)}) copy-start(f32[4,256,64]{1,2,0:T(8,128)} %param.15) | copy-start | bytes 786436
  55.7 158.7 %all-reduce.12.cloned.1.call-start = ((), (), s32[]{:S(2)}) async-start(), calls=%async_computation.2 | async-start | bytes 262144 | tf_op jit(solution)/shard_map/psum | solution.py:29
  108.6 62.4 %copy-start = (f32[256,64]{0,1:T(8,128)S(1)}, f32[256,64]{0,1:T(8,128)}, u32[]{:S(2)}) copy-start(f32[256,64]{0,1:T(8,128)} %all-reduce.10.cloned.1.call-done) | copy-start | bytes 196612
  173.0 109.0 %all-reduce.14.cloned.1.call-start = ((), (), s32[]{:S(2)}) async-start(), calls=%async_computation.3 | async-start | bytes 131072 | tf_op jit(solution)/shard_map/psum | solution.py:120
  214.5 7.2 copy-start.5
  227.2 161.1 %all-reduce.16.cloned.1.call-start = ((), (), s32[]{:S(2)}) async-start(), calls=%async_computation.4 | async-start | bytes 262144 | tf_op jit(solution)/shard_map/psum | solution.py:29
  282.1 62.8 %copy-start.2 = (f32[256,64]{0,1:T(8,128)S(1)}, f32[256,64]{0,1:T(8,128)}, u32[]{:S(2)}) copy-start(f32[256,64]{0,1:T(8,128)} %all-reduce.14.cloned.1.call-done) | copy-start | bytes 196612
  346.9 109.0 %all-reduce.18.cloned.1.call-start = ((), (), s32[]{:S(2)}) async-start(), calls=%async_computation.5 | async-start | bytes 131072 | tf_op jit(solution)/shard_map/psum | solution.py:120
  388.3 7.2 copy-start.6
  401.1 161.1 %all-reduce.20.cloned.1.call-start = ((), (), s32[]{:S(2)}) async-start(), calls=%async_computation.6 | async-start | bytes 262144 | tf_op jit(solution)/shard_map/psum | solution.py:29
  455.9 62.7 %copy-start.3 = (f32[256,64]{0,1:T(8,128)S(1)}, f32[256,64]{0,1:T(8,128)}, u32[]{:S(2)}) copy-start(f32[256,64]{0,1:T(8,128)} %all-reduce.18.cloned.1.call-done) | copy-start | bytes 196612
  520.7 109.1 %all-reduce.22.cloned.1.call-start = ((), (), s32[]{:S(2)}) async-start(), calls=%async_computation.7 | async-start | bytes 131072 | tf_op jit(solution)/shard_map/psum | solution.py:120
  562.2 7.2 copy-start.7
  574.9 161.1 %all-reduce.24.cloned.1.call-start = ((), (), s32[]{:S(2)}) async-start(), calls=%async_computation.8 | async-start | bytes 262144 | tf_op jit(solution)/shard_map/psum | solution.py:29
  629.8 62.8 %copy-start.1 = (f32[256,64]{0,1:T(8,128)S(1)}, f32[256,64]{0,1:T(8,128)}, u32[]{:S(2)}) copy-start(f32[256,64]{0,1:T(8,128)} %all-reduce.22.cloned.1.call-done) | copy-start | bytes 196612
  736.0 7.2 copy-start.8
Sparse Core Ops, SparseCore 0:
  55.9 52.6 all-reduce.9
  173.2 41.2 all-reduce.11
  227.4 54.6 all-reduce.13
  347.0 41.2 all-reduce.15
  401.2 54.6 all-reduce.17
  520.8 41.2 all-reduce.19
  575.0 54.6 all-reduce.21
  694.7 41.2 all-reduce.23
where the time goes:
time: 760 us; the launch traced here: 755 us
  waiting for transfers between devices  404 us (53%)
  other arithmetic  227 us (30%)
  matrix products  64 us (8%)
  between operations  25.2 us (3%)
  local copies, waits for them, and re-layouts  22.6 us (3%)
  starting transfers between devices  10.3 us (1%)
    psum x4, waiting for transfers between devices, on_device(): observed = lax.psum(partial_obs, 'member')  213 us
    psum x4, waiting for transfers between devices, spread_2(): return lax.psum(jnp.where(mine, shard, jnp.zeros_like(shard)), axis)  166 us
    another operation x27, other arithmetic, solve_batch(): factor = jnp.linalg.cholesky(system)  138 us
    another operation x9, other arithmetic, solve_batch(): lax.linalg.triangular_solve(factor, forward, left_side=True, lower=True,...  78.8 us
    dot_general x4, matrix products, apply_batch(): lax.dot_general(anomaly, spread, (((0,), (1,)), ((), ())), precision=lax....  28.9 us
    all_to_all x1, waiting for transfers between devices, on_device(): lax.all_to_all(unrolled_array, 'member', split_axis=1, concat_axis=0, til...  20.8 us
    another operation x29, local copies, waits for them, and re-layouts, solve_batch(): lax.linalg.triangular_solve(factor, forward, left_side=True, lower=True,...  15.7 us
  transfers between devices with their start and end apart: 11, of which 11 were waited for; matrix products, arithmetic and copies ran while one was open for 0% of the time, Pallas kernels for 0%

commit v1 on v0

v1 whole, which is shorter than its diff:
```python
import functools
import math

import jax
import jax.numpy as jnp
from jax import lax
from jax.experimental import pallas as pl
from jax.experimental.pallas import tpu as pltpu
from jax.sharding import PartitionSpec as P

COURANT = 0.3
ROTATION = 0.1
HALF = COURANT * 0.5
F32 = jnp.float32
BF16 = jnp.bfloat16
VMEM_SPEC = pl.BlockSpec(memory_space=pltpu.VMEM)
SMEM_SPEC = pl.BlockSpec(memory_space=pltpu.SMEM)


def d_y(field):
    width = field.shape[-1]
    axis = field.ndim - 1
    return (pltpu.roll(field, width - 1, axis) - pltpu.roll(field, 1, axis)) * 0.5


def split2(x):
    high = x.astype(BF16)
    return high, (x - high.astype(F32)).astype(BF16)


def mm(a, b):
    return lax.dot_general(a, b, (((1,), (0,)), ((), ())), preferred_element_type=F32)


def mm_f32(a, b, dims=((1,), (0,))):
    return lax.dot_general(
        a, b, (dims, ((), ())), precision=lax.Precision.HIGHEST, preferred_element_type=F32
    )


def keep_lanes(ref, start, value):
    rows, width = value.shape
    for c in range(width // 128):
        ref[c, start : start + rows, :] = value[:, c * 128 : (c + 1) * 128]


def every_nth(ref, start, count, stride):
    return jnp.concatenate(
        [ref[c, pl.ds(start, count, stride=stride), :] for c in range(ref.shape[0])], axis=1)


def row_up(field, edge, index):
    rows = field.shape[0]
    return jnp.where(index == rows - 1, edge, pltpu.roll(field, rows - 1, 0))


def row_down(field, edge, index):
    return jnp.where(index == 0, edge, pltpu.roll(field, 1, 0))


def wave_twice(h, u, v, low, high, velocities):
    rows = h.shape[0]
    index = lax.broadcasted_iota(jnp.int32, h.shape, 0)
    u_low, q_low, r_low, s_low = low
    u_high, q_high, r_high, s_high = high
    h1 = h - HALF * (row_up(u, u_high, index) - row_down(u, u_low, index)) - COURANT * d_y(v)
    h1_low = q_low - HALF * u[0:1]
    h1_high = q_high + HALF * u[rows - 1 : rows]
    u1 = u - HALF * (row_up(h1, h1_high, index) - row_down(h1, h1_low, index)) + ROTATION * v
    v1 = v - COURANT * d_y(h1) - ROTATION * u
    u1_low = r_low - HALF * h1[0:1]
    u1_high = r_high + HALF * h1[rows - 1 : rows]
    h2 = h1 - HALF * (row_up(u1, u1_high, index) - row_down(u1, u1_low, index)) - COURANT * d_y(v1)
    if not velocities:
        return h2
    keep = 1.0 - HALF * HALF
    square = COURANT * COURANT
    h2_low = keep * h1_low + square * d_y(d_y(h1_low)) + s_low - HALF * u1[0:1]
    h2_high = keep * h1_high + square * d_y(d_y(h1_high)) + s_high + HALF * u1[rows - 1 : rows]
    u2 = u1 - HALF * (row_up(h2, h2_high, index) - row_down(h2, h2_low, index)) + ROTATION * v1
    v2 = v1 - COURANT * d_y(h2) - ROTATION * u1
    return h2, u2, v2


def edge_rows(h, u, v, sign):
    a = sign * HALF
    dv0 = COURANT * d_y(v[0])
    q = h[0] + a * u[1] - dv0
    h1_1 = h[1] - a * (u[0] - u[2]) - COURANT * d_y(v[1])
    r = u[0] + a * h1_1 + ROTATION * v[0]
    h1_2 = h[2] - a * (u[1] - u[3]) - COURANT * d_y(v[2])
    p = u[1] + a * h1_2 + ROTATION * v[1]
    s = a * p - dv0 + COURANT * ROTATION * d_y(u[0])
    h1 = a * u[0]
    first = (1.0 - 2.0 * HALF * HALF) * h1 + a * r + COURANT * COURANT * d_y(d_y(h1))
    return (u[0], q, r, s), (first, HALF * HALF * q, HALF * HALF * h1)


def prior_kernel(members, cells_x, slabs, batches, me_ref, owner_ref, x_ref, offset_ref,
                 obs_ref, low_ref, high_ref, rows_ref, lanes_ref):
    cells_y = x_ref.shape[1]
    nobs = offset_ref.shape[1]
    zero = (jnp.zeros((1, cells_y), F32),) * 4
    base = members * cells_x
    for m in range(members):
        start = m * 3 * cells_x
        h, u, v = (x_ref[pl.ds(start + f * cells_x, cells_x), :] for f in range(3))
        rows_ref[pl.ds(m * cells_x, cells_x), :] = wave_twice(h, u, v, zero, zero, False)

    keep_lanes(lanes_ref, 0, x_ref[...])

    def across(field, row):
        return every_nth(lanes_ref, field * cells_x + row, members, 3 * cells_x)

    last = cells_x - 1
    sent, added = edge_rows(
        [across(0, last - i) for i in range(3)], [across(1, last - i) for i in range(4)],
        [across(2, last - i) for i in range(3)], 1.0)
    for i in range(4):
        low_ref[pl.ds(i * members, members), :] = sent[i]
    for i in range(3):
        rows_ref[pl.ds(base + i * members, members), :] = added[i]
    sent, added = edge_rows(
        [across(0, i) for i in range(3)], [across(1, i) for i in range(4)],
        [across(2, i) for i in range(3)], -1.0)
    for i in range(4):
        high_ref[pl.ds(i * members, members), :] = sent[i]
    for i in range(3):
        rows_ref[pl.ds(base + (3 + i) * members, members), :] = added[i]

    values = rows_ref[...]
    part0 = values.astype(BF16)
    rest = values - part0.astype(F32)
    part1 = rest.astype(BF16)
    part2 = (rest - part1.astype(F32)).astype(BF16)
    me = me_ref[0]
    total = cells_x * slabs
    for b in range(batches):
        offset = offset_ref[b : b + 1, :]
        column = lax.rem(offset, cells_y)
        row = lax.div(offset, cells_y)
        relative = row + lax.rem(owner_ref[b % slabs] - me + slabs, slabs) * cells_x
        pick = jnp.where(
            lax.broadcasted_iota(jnp.int32, (cells_y, nobs), 0) == column, 1.0, 0.0).astype(BF16)
        found = mm(part0, pick) + (mm(part1, pick) + mm(part2, pick))
        inside = lax.broadcasted_iota(jnp.int32, (cells_x, nobs), 0) == relative
        edges = jnp.zeros((members, nobs), F32)
        for i in range(3):
            piece = found[base + i * members : base + (i + 1) * members]
            edges += jnp.where(relative == cells_x + i, piece, 0.0)
            piece = found[base + (3 + i) * members : base + (4 + i) * members]
            edges += jnp.where(relative == total - 1 - i, piece, 0.0)
        own = [
            jnp.sum(jnp.where(inside, found[m * cells_x : (m + 1) * cells_x], 0.0),
                    axis=0, keepdims=True)
            for m in range(members)
        ]
        obs_ref[:, b * nobs : (b + 1) * nobs] = jnp.concatenate(own, axis=0) + edges


def forecast_kernel(members, cells_x, x_ref, low_ref, high_ref, out_ref, rows_ref):
    cells_y = x_ref.shape[1]
    chunk = out_ref.shape[2]
    piece = math.gcd(chunk, cells_y)
    for m in range(members):
        start = m * 3 * cells_x
        h, u, v = (x_ref[pl.ds(start + f * cells_x, cells_x), :] for f in range(3))
        low = [low_ref[pl.ds(i * members + m, 1), :] for i in range(4)]
        high = [high_ref[pl.ds(i * members + m, 1), :] for i in range(4)]
        for f, value in enumerate(wave_twice(h, u, v, low, high, True)):
            keep_lanes(rows_ref, start + f * cells_x, value)
    for r in range(cells_x):
        for f in range(3):
            line = every_nth(rows_ref, f * cells_x + r, members, 3 * cells_x)
            for c in range(0, cells_y, piece):
                flat = (r * 3 + f) * cells_y + c
                out_ref[flat // chunk, :, flat % chunk : flat % chunk + piece] = line[:, c : c + piece]


def column_of(row):
    return jnp.transpose(jnp.broadcast_to(row, (8,) + row.shape[1:]))[:, 0:1]


def taper_of(row_i, column_i, inverse_i, row_j, column_j, total_x, cells_y):
    gap_x = jnp.abs(row_j - row_i)
    gap_x = jnp.minimum(gap_x, total_x - gap_x)
    gap_y = jnp.abs(column_j - column_i)
    gap_y = jnp.minimum(gap_y, cells_y - gap_y)
    distance = jnp.sqrt(gap_x * gap_x + gap_y * gap_y)
    ramp = jnp.maximum(0.0, 1.0 - distance * inverse_i)
    return ramp * ramp


def geometry(owner_ref, offset_ref, cutoff_ref, b, slabs, cells_x, cells_y):
    offset = offset_ref[b : b + 1, :]
    row = lax.div(offset, cells_y) + owner_ref[b % slabs] * cells_x
    column = lax.rem(offset, cells_y)
    return row.astype(F32), column.astype(F32), 1.0 / cutoff_ref[b : b + 1, :].astype(F32)


def taper_kernel(slabs, cells_x, cells_y, batches, tile, groups, first_ref, owner_ref, offset_ref,
                 cutoff_ref, out_ref):
    nobs = offset_ref.shape[1]
    for b in range(batches):
        row, column, inverse = geometry(owner_ref, offset_ref, cutoff_ref, b, slabs, cells_x, cells_y)
        row, column, inverse = column_of(row), column_of(column), column_of(inverse)
        for g, at in enumerate(groups):
            start = first_ref[0] + at
            cell_row = lax.div(start, 3 * cells_y).astype(F32)
            cell_column = (lax.rem(start, cells_y) + lax.broadcasted_iota(jnp.int32, (1, tile), 1)).astype(F32)
            out_ref[b, g] = taper_of(row, column, inverse, cell_row, cell_column,
                                     float(cells_x * slabs), float(cells_y))


def chain_kernel(slabs, cells_x, cells_y, batches, parts, *refs):
    place_ref, owner_ref, offset_ref, cutoff_ref, values_ref, variance_ref, perturb_ref = refs[:7]
    part_refs = refs[7 : 7 + parts]
    y_ref, w_ref, obs_ref, aug_ref = refs[7 + parts :]
    members = obs_ref.shape[0]
    nobs = offset_ref.shape[1]
    each = part_refs[0].shape[0]
    scale = 1.0 / (members - 1)
    for k in range(parts):
        obs_ref[pl.ds(pl.multiple_of(place_ref[k] * each, each), each), :] = part_refs[k][...]
    eye = (lax.broadcasted_iota(jnp.int32, (members, members), 0)
           == lax.broadcasted_iota(jnp.int32, (members, members), 1))
    places = [geometry(owner_ref, offset_ref, cutoff_ref, b, slabs, cells_x, cells_y)
              for b in range(batches)]
    sublane = lax.broadcasted_iota(jnp.int32, (8, 2 * members), 0)
    for b in range(batches):
        observed = obs_ref[:, b * nobs : (b + 1) * nobs]
        spread = observed - jnp.mean(observed, axis=0, keepdims=True)
        variance = variance_ref[b : b + 1, :]
        inverse = 1.0 / variance
        target = values_ref[b : b + 1, :] + jnp.sqrt(variance) * perturb_ref[b] - observed
        both = mm_f32(spread * inverse, jnp.concatenate([spread, target], axis=0), ((1,), (1,)))
        gram = both[:, :members] + jnp.where(eye, float(members - 1), 0.0)
        aug_ref[:, :members] = gram
        aug_ref[:, members:] = both[:, members:]

        def eliminate(block, carry):
            at = pl.ds(pl.multiple_of(block * 8, 8), 8)
            panel = aug_ref[at, :]
            for j in range(8):
                line = panel[j : j + 1, :] * (1.0 / panel[j : j + 1, j : j + 1])
                panel = jnp.where(sublane == j, line, panel - panel[:, j : j + 1] * line)
            every = aug_ref[...]
            for j in range(8):
                every = every - every[:, j : j + 1] * panel[j : j + 1, :] if j == 0 else every - aug_ref[:, j : j + 1] * panel[j : j + 1, :]
            aug_ref[...] = every
            aug_ref[at, :] = panel
            aug_ref[...] = pltpu.roll(aug_ref[...], 2 * members - 8, 1)
            return carry

        lax.fori_loop(0, members // 8, eliminate, 0)
        solved = aug_ref[:, :members]
        weights = (target - mm_f32(solved, spread, ((0,), (0,)))) * inverse
        spread_t = jnp.transpose(spread) * scale
        high, low = split2(spread_t)
        y_ref[b] = jnp.concatenate([high, high, low], axis=1)
        high, low = split2(weights)
        w_ref[b] = jnp.concatenate([high, low], axis=0)
        if b + 1 < batches:
            later = obs_ref[:, (b + 1) * nobs :]
            anomaly = later - jnp.mean(later, axis=0, keepdims=True)
            covariance = mm_f32(spread_t, anomaly)
            row, column, inverse_cutoff = (column_of(x) for x in places[b])
            row_j = jnp.concatenate([places[c][0] for c in range(b + 1, batches)], axis=1)
            column_j = jnp.concatenate([places[c][1] for c in range(b + 1, batches)], axis=1)
            taper = taper_of(row, column, inverse_cutoff, row_j, column_j,
                             float(cells_x * slabs), float(cells_y))
            obs_ref[:, (b + 1) * nobs :] = later + mm_f32(weights, covariance * taper)


def update_kernel(batches, tile, groups, s_ref, y_ref, w_ref, taper_ref, out_ref):
    members = s_ref.shape[0]
    for g, tiles in enumerate(groups):
        state = jnp.concatenate([s_ref[:, at : at + tile] for at in tiles], axis=1)
        for b in range(batches):
            anomaly = state - jnp.mean(state, axis=0, keepdims=True)
            high, low = split2(anomaly)
            covariance = mm(y_ref[b], jnp.concatenate([high, low, high], axis=0))
            taper = taper_ref[b, g]
            gain = covariance * jnp.concatenate([taper] * len(tiles), axis=1)
            high, low = split2(gain)
            two = mm(w_ref[b], high)
            one = mm(w_ref[b, :members], low)
            state = state + (two[:members] + (two[members:] + one))
        for i, at in enumerate(tiles):
            out_ref[:, at : at + tile] = state[:, i * tile : (i + 1) * tile]


def on_device(prior, obs_values, obs_variance, obs_perturb, obs_offset, owner_order, taper_cutoff):
    slabs = lax.axis_size("slab")
    shards = lax.axis_size("member")
    each, cells_x, _, cells_y = prior.shape
    batches, nobs = obs_values.shape
    members = each * shards
    chunk = 3 * cells_x * cells_y // shards
    slab = lax.axis_index("slab")
    member = lax.axis_index("member")
    x = prior.transpose(0, 2, 1, 3).reshape(each * 3 * cells_x, cells_y)
    owner = owner_order.astype(jnp.int32)
    perturb = obs_perturb.transpose(0, 2, 1)

    def shift(count, by):
        return [(i, (i + by) % count) for i in range(count)]

    partial, low, high = pl.pallas_call(
        functools.partial(prior_kernel, each, cells_x, slabs, batches),
        out_shape=(
            jax.ShapeDtypeStruct((each, batches * nobs), F32),
            jax.ShapeDtypeStruct((4 * each, cells_y), F32),
            jax.ShapeDtypeStruct((4 * each, cells_y), F32),
        ),
        in_specs=[SMEM_SPEC, SMEM_SPEC, VMEM_SPEC, VMEM_SPEC],
        out_specs=(VMEM_SPEC,) * 3,
        scratch_shapes=[
            pltpu.VMEM((each * cells_x + 6 * each, cells_y), F32),
            pltpu.VMEM((cells_y // 128, each * 3 * cells_x, 128), F32),
        ],
        name="prior",
    )(slab.reshape(1), owner, x, obs_offset)

    observed = partial
    for by in range(1, slabs):
        observed = observed + lax.ppermute(partial, "slab", shift(slabs, by))
    low = lax.ppermute(low, "slab", shift(slabs, 1))
    high = lax.ppermute(high, "slab", shift(slabs, -1))

    pieces = [observed]
    for by in range(1, shards):
        pieces.append(lax.ppermute(observed, "member", shift(shards, by)))
    place = lax.rem(member - jnp.arange(shards, dtype=jnp.int32) + shards, shards)

    outgoing = pl.pallas_call(
        functools.partial(forecast_kernel, each, cells_x),
        out_shape=jax.ShapeDtypeStruct((shards, each, chunk), F32),
        in_specs=[VMEM_SPEC] * 3,
        out_specs=VMEM_SPEC,
        scratch_shapes=[pltpu.VMEM((cells_y // 128, each * 3 * cells_x, 128), F32)],
        name="forecast",
    )(x, low, high)
    state = lax.all_to_all(outgoing, "member", 0, 0).reshape(members, chunk)

    tile = math.gcd(chunk, 256)
    if chunk % (3 * cells_y) == 0:
        groups = [
            [r * 3 * cells_y + f * cells_y + c for f in range(3)]
            for r in range(chunk // (3 * cells_y))
            for c in range(0, cells_y, tile)
        ]
    else:
        groups = [[at] for at in range(0, chunk, tile)]
    first = (slab * shards + member) * chunk
    taper = pl.pallas_call(
        functools.partial(taper_kernel, slabs, cells_x, cells_y, batches, tile, [g[0] for g in groups]),
        out_shape=jax.ShapeDtypeStruct((batches, len(groups), nobs, tile), F32),
        in_specs=[SMEM_SPEC, SMEM_SPEC, VMEM_SPEC, VMEM_SPEC],
        out_specs=VMEM_SPEC,
        name="taper",
    )(first.reshape(1), owner, obs_offset, taper_cutoff)

    y_all, w_all = pl.pallas_call(
        functools.partial(chain_kernel, slabs, cells_x, cells_y, batches, shards),
        out_shape=(
            jax.ShapeDtypeStruct((batches, nobs, 3 * members), BF16),
            jax.ShapeDtypeStruct((batches, 2 * members, nobs), BF16),
        ),
        in_specs=[SMEM_SPEC, SMEM_SPEC] + [VMEM_SPEC] * (5 + shards),
        out_specs=(VMEM_SPEC,) * 2,
        scratch_shapes=[
            pltpu.VMEM((members, batches * nobs), F32),
            pltpu.VMEM((members, 2 * members), F32),
        ],
        name="chain",
    )(place, owner, obs_offset, taper_cutoff, obs_values, obs_variance, perturb, *pieces)

    return pl.pallas_call(
        functools.partial(update_kernel, batches, tile, groups),
        out_shape=jax.ShapeDtypeStruct((members, chunk), F32),
        in_specs=[VMEM_SPEC] * 4,
        out_specs=VMEM_SPEC,
        name="update",
    )(state, y_all, w_all, taper)


def solution(mesh):
    in_specs = (P("member", "slab", None, None), P(), P(), P(), P(), P(), P())
    out_specs = P(None, ("slab", "member"))
    return jax.shard_map(
        on_device, mesh=mesh, in_specs=in_specs, out_specs=out_specs, check_vma=False
    )
```

time: 760 us -> 96.8 us (0.13)
  waiting for transfers between devices: 404 us -> 8.98 us
  other arithmetic: 227 us -> 1.35 us
  matrix products: 64 us -> 0 us
  Pallas kernels: 0 us -> 54.8 us
  between operations: 25.2 us -> 0.13 us
  local copies, waits for them, and re-layouts: 22.6 us -> 2.1 us
  starting transfers between devices: 10.3 us -> 28.3 us
    psum x8 -> x0, waiting for transfers between devices: 379 us -> none  [the longest x4 213 us: on_device(): observed = lax.psum(partial_obs, 'member')]
    another operation x46 -> x0, other arithmetic: 217 us -> none  [the longest x27 138 us: solve_batch(): factor = jnp.linalg.cholesky(system)]
    dot_general x16 -> x0, matrix products: 57 us -> none  [the longest x4 28.9 us: apply_batch(): lax.dot_general(anomaly, spread, (((0,), (1,)), ((), ())), precision=lax....]
    pallas_call x0 -> x5, Pallas kernels: none -> 54.8 us  [the longest x1 31 us: on_device(): pl.pallas_call(functools.partial(chain_kernel, slabs, cells_x, cells_y, b...]
    all_to_all x1, waiting for transfers between devices: 20.8 us -> 0.01 us  [on_device(): state = lax.all_to_all(outgoing, 'member', 0, 0).reshape(members, chunk)]
    ppermute x2 -> x12, starting transfers between devices: 4.04 us -> 23.3 us  [the longest x7 16.1 us: on_device(): pieces.append(lax.ppermute(observed, 'member', shift(shards, by)))]
    another operation x38 -> x0, local copies, waits for them, and re-layouts: 16.3 us -> none  [the longest x29 15.7 us: solve_batch(): lax.linalg.triangular_solve(factor, forward, left_side=True, lower=True,...]
  transfers between devices with their start and end apart: 11 -> 13, of which waited for: 11 -> 5; matrix products, arithmetic and copies ran while one was open for 0% -> 1% of each run, Pallas kernels for 0% -> 38%
where the time goes in v1:
time: 96.8 us; the launch traced here: 95.7 us
  Pallas kernels  54.8 us (57%)
  starting transfers between devices  28.3 us (29%)
  waiting for transfers between devices  8.98 us (9%)
  local copies, waits for them, and re-layouts  2.1 us (2%)
  other arithmetic  1.35 us (1%)
    pallas_call x1, Pallas kernels, on_device(): pl.pallas_call(functools.partial(chain_kernel, slabs, cells_x, cells_y, b...  31 us
    ppermute x7, starting transfers between devices, on_device(): pieces.append(lax.ppermute(observed, 'member', shift(shards, by)))  16.1 us
    pallas_call x1, Pallas kernels, on_device(): pl.pallas_call(functools.partial(update_kernel, batches, tile, groups), o...  10.2 us
    pallas_call x1, Pallas kernels, on_device(): pl.pallas_call(functools.partial(taper_kernel, slabs, cells_x, cells_y, b...  5.68 us
    all_to_all x1, starting transfers between devices, on_device(): state = lax.all_to_all(outgoing, 'member', 0, 0).reshape(members, chunk)  5.04 us
    ppermute x3, waiting for transfers between devices, on_device(): observed = observed + lax.ppermute(partial, 'slab', shift(slabs, by))  5.02 us
    pallas_call x1, Pallas kernels, on_device(): pl.pallas_call(functools.partial(forecast_kernel, each, cells_x), out_sha...  4.69 us
    ppermute x3, starting transfers between devices, on_device(): observed = observed + lax.ppermute(partial, 'slab', shift(slabs, by))  3.26 us
  transfers between devices with their start and end apart: 13, of which 5 were waited for; matrix products, arithmetic and copies ran while one was open for 1% of the time, Pallas kernels for 38%

profile of v1, /device:TPU:0, one launch (start us, length us, event | category | flops | bytes accessed | tf_op | source)
XLA Modules:
  0.0 95.7 jit_solution(17130834090305951976)
XLA Ops:
  0.0 3.2 %prior.1 = (f32[8,1024]{1,0:T(8,128)}, f32[32,512]{1,0:T(8,128)}, f32[32,512]{1,0:T(8,128)}) custom-call(s32[1]{0:T(128)} %bitcast.2.me_ref, s32[4]{0:T(128)} %owner_ref.3, f32[384,512]{1,0:T(8,128)} %bitcast.8, s32[4,256]{1,0:T(4,128)} %offset_ref.3), custom_call_target="tpu_custom_call" | custom-call | tf_op jit(solution)/shard_map/prior/pallas_call | solution.py:309
  3.2 3.0 %collective-permute-start = (f32[32,512]{1,0:T(8,128)}, f32[32,512]{1,0:T(8,128)S(1)}, u32[]{:S(2)}, u32[]{:S(2)}) collective-permute-start(f32[32,512]{1,0:T(8,128)} %get-tuple-element.10), channel_id=1, source_target_pairs={{0,8},{8,16},{16,24},{24,0},{1,9},{9,17},{17,25},{25,1},{2,10},{10... | collective-permute-start | bytes 196616 | tf_op jit(solution)/shard_map/ppermute | solution.py:328
  6.2 1.0 %collective-permute-start.1 = (f32[32,512]{1,0:T(8,128)}, f32[32,512]{1,0:T(8,128)S(1)}, u32[]{:S(2)}, u32[]{:S(2)}) collective-permute-start(f32[32,512]{1,0:T(8,128)} %get-tuple-element.11), channel_id=1, source_target_pairs={{0,24},{8,0},{16,8},{24,16},{1,25},{9,1},{17,9},{25,17},{2,26},{10... | collective-permute-start | bytes 196616 | tf_op jit(solution)/shard_map/ppermute | solution.py:329
  7.2 2.5 %collective-permute-done.low_ref = f32[32,512]{1,0:T(8,128)S(1)} collective-permute-done((f32[32,512]{1,0:T(8,128)}, f32[32,512]{1,0:T(8,128)S(1)}, u32[]{:S(2)}, u32[]{:S(2)}) %collective-permute-start) | collective-permute-done | bytes 65568 | tf_op jit(solution)/shard_map/ppermute | solution.py:328
  9.7 0.0 copy-start.2
  9.7 1.4 %collective-permute-done.1.high_ref = f32[32,512]{1,0:T(8,128)S(1)} collective-permute-done((f32[32,512]{1,0:T(8,128)}, f32[32,512]{1,0:T(8,128)S(1)}, u32[]{:S(2)}, u32[]{:S(2)}) %collective-permute-start.1) | collective-permute-done | bytes 65568 | tf_op jit(solution)/shard_map/ppermute | solution.py:329
  11.1 0.0 copy-done.2
  11.1 0.0 copy-start.3
  11.1 0.6 copy-done.3
  11.8 4.7 %forecast.1 = f32[8,8,3072]{2,1,0:T(8,128)} custom-call(f32[384,512]{1,0:T(8,128)} %bitcast.9, f32[32,512]{1,0:T(8,128)} %copy-done.2, f32[32,512]{1,0:T(8,128)} %copy-done.3), custom_call_target="tpu_custom_call" | custom-call | tf_op jit(solution)/shard_map/forecast/pallas_call | solution.py:336
  16.4 5.0 %all-to-all-start = ((f32[8,8,3072]{2,1,0:T(8,128)}), f32[8,8,3072]{2,1,0:T(8,128)S(1)}, u32[]{:S(2)}, u32[]{:S(2)}) async-start(f32[8,8,3072]{2,1,0:T(8,128)} %forecast.1), calls=%async_computation | async-start | bytes 1572864 | tf_op jit(solution)/shard_map/all_to_all | solution.py:344
  21.5 1.7 %collective-permute-start.4 = (f32[8,1024]{1,0:T(8,128)}, f32[8,1024]{1,0:T(8,128)S(1)}, u32[]{:S(2)}, u32[]{:S(2)}) collective-permute-start(f32[8,1024]{1,0:T(8,128)} %get-tuple-element.12), channel_id=1, source_target_pairs={{0,24},{8,0},{16,8},{24,16},{1,25},{9,1},{17,9},{25,17},{2,26},{10... | collective-permute-start | bytes 98312 | tf_op jit(solution)/shard_map/ppermute | solution.py:327
  23.2 1.5 %collective-permute-start.3 = (f32[8,1024]{1,0:T(8,128)}, f32[8,1024]{1,0:T(8,128)S(1)}, u32[]{:S(2)}, u32[]{:S(2)}) collective-permute-start(f32[8,1024]{1,0:T(8,128)} %get-tuple-element.12), channel_id=1, source_target_pairs={{0,16},{8,24},{16,0},{24,8},{1,17},{9,25},{17,1},{25,9},{2,18},{10... | collective-permute-start | bytes 98312 | tf_op jit(solution)/shard_map/ppermute | solution.py:327
  24.7 0.0 collective-permute-start.2
  24.7 0.9 collective-permute-done.4
  25.6 1.7 %collective-permute-done.3 = f32[8,1024]{1,0:T(8,128)S(1)} collective-permute-done((f32[8,1024]{1,0:T(8,128)}, f32[8,1024]{1,0:T(8,128)S(1)}, u32[]{:S(2)}, u32[]{:S(2)}) %collective-permute-start.3) | collective-permute-done | bytes 32800 | tf_op jit(solution)/shard_map/ppermute | solution.py:327
  27.4 2.4 %collective-permute-done.2 = f32[8,1024]{1,0:T(8,128)S(1)} collective-permute-done((f32[8,1024]{1,0:T(8,128)}, f32[8,1024]{1,0:T(8,128)S(1)}, u32[]{:S(2)}, u32[]{:S(2)}) %collective-permute-start.2) | collective-permute-done | bytes 32800 | tf_op jit(solution)/shard_map/ppermute | solution.py:327
  29.8 0.8 add_add_fusion.refs_7_
  30.5 0.0 copy-start.1
  30.6 2.2 %collective-permute-start.11 = (f32[8,1024]{1,0:T(8,128)S(1)}, f32[8,1024]{1,0:T(8,128)S(1)}, u32[]{:S(2)}, u32[]{:S(2)}) collective-permute-start(f32[8,1024]{1,0:T(8,128)S(1)} %add_add_fusion.refs_7_), channel_id=1, source_target_pairs={{0,7},{1,0},{2,1},{3,2},{4,3},{5,4},{6,5},{7,6},{8,15},{9,8},{10,9... | collective-permute-start | bytes 98312 | tf_op jit(solution)/shard_map/ppermute | solution.py:333
  32.7 1.8 %collective-permute-start.10 = (f32[8,1024]{1,0:T(8,128)S(1)}, f32[8,1024]{1,0:T(8,128)S(1)}, u32[]{:S(2)}, u32[]{:S(2)}) collective-permute-start(f32[8,1024]{1,0:T(8,128)S(1)} %add_add_fusion.refs_7_), channel_id=1, source_target_pairs={{0,6},{1,7},{2,0},{3,1},{4,2},{5,3},{6,4},{7,5},{8,14},{9,15},{10,... | collective-permute-start | bytes 98312 | tf_op jit(solution)/shard_map/ppermute | solution.py:333
  34.5 0.0 collective-permute-start.9
  34.5 2.7 %collective-permute-start.8 = (f32[8,1024]{1,0:T(8,128)S(1)}, f32[8,1024]{1,0:T(8,128)S(1)}, u32[]{:S(2)}, u32[]{:S(2)}) collective-permute-start(f32[8,1024]{1,0:T(8,128)S(1)} %add_add_fusion.refs_7_), channel_id=1, source_target_pairs={{0,4},{1,5},{2,6},{3,7},{4,0},{5,1},{6,2},{7,3},{8,12},{9,13},{10,... | collective-permute-start | bytes 98312 | tf_op jit(solution)/shard_map/ppermute | solution.py:333
  37.2 0.0 collective-permute-start.7
  37.2 0.0 collective-permute-done.11.refs_14_
  37.2 0.0 copy-start.4
  37.2 0.8 collective-permute-start.6
  38.0 0.0 collective-permute-done.10.refs_13_
  38.0 0.0 copy-start.5
  38.0 8.6 %collective-permute-start.5 = (f32[8,1024]{1,0:T(8,128)S(1)}, f32[8,1024]{1,0:T(8,128)S(1)}, u32[]{:S(2)}, u32[]{:S(2)}) collective-permute-start(f32[8,1024]{1,0:T(8,128)S(1)} %add_add_fusion.refs_7_), channel_id=1, source_target_pairs={{0,1},{1,2},{2,3},{3,4},{4,5},{5,6},{6,7},{7,0},{8,9},{9,10},{10,1... | collective-permute-start | bytes 98312 | tf_op jit(solution)/shard_map/ppermute | solution.py:333
  46.6 0.6 compare_select_fusion.refs_0_
  47.2 5.7 %taper.1.taper_ref = f32[4,4,256,256]{3,2,1,0:T(8,128)} custom-call(s32[1]{0:T(128)} %bitcast.6.first_ref, s32[4]{0:T(128)} %owner_ref.3, s32[4,256]{1,0:T(4,128)} %offset_ref.3, s32[4,256]{1,0:T(4,128)} %cutoff_ref.1), custom_call_target="tpu_custom_call" | custom-call | tf_op jit(solution)/shard_map/taper/pallas_call | solution.py:356
  52.9 0.0 collective-permute-done.9.refs_12_
  52.9 0.0 copy-start.6
  52.9 0.0 collective-permute-done.8.refs_11_
  52.9 0.0 copy-start.7
  52.9 0.0 collective-permute-done.7.refs_10_
  52.9 0.0 copy-start.8
  52.9 0.0 collective-permute-done.6.refs_9_
  52.9 0.0 copy-start.9
  53.0 0.0 collective-permute-done.5.refs_8_
  53.0 0.0 copy-start.10
  53.0 0.0 copy-done.1
  53.0 0.0 copy-done.4
  53.0 0.0 copy-done.5
  53.0 0.5 copy-done.6
  53.5 0.0 copy-done.7
  53.5 0.0 copy-done.8
  53.5 0.0 copy-done.9
  53.6 0.0 copy-done.10
  53.6 31.0 %chain.1 = (bf16[4,256,192]{2,1,0:T(8,128)(2,1)}, bf16[4,128,256]{2,1,0:T(8,128)(2,1)}) custom-call(s32[8]{0:T(128)} %compare_select_fusion.refs_0_, s32[4]{0:T(128)} %owner_ref.3, s32[4,256]{1,0:T(4,128)} %offset_ref.3, s32[4,256]{1,0:T(4,128)} %cutoff_ref.1, f32[4,256]{1,0:T(4,128)} %refs_4_.1, f32[4,256]{1,0:T(4,128)} %refs_5_.1, f32[4,64,256]{2,1,0:T(8,128)} %bitcast.10, ...), custom_call_target="tpu_custom_call" | custom-call | tf_op jit(solution)/shard_map/chain/pallas_call | solution.py:364
  84.6 0.0 all-to-all-done
  84.6 0.0 copy-start
  84.6 0.9 copy-done
  85.5 10.2 %update.1 = f32[64,3072]{1,0:T(8,128)} custom-call(f32[64,3072]{1,0:T(8,128)} %bitcast.7, bf16[4,256,192]{2,1,0:T(8,128)(2,1)} %get-tuple-element.13.y_ref, bf16[4,128,256]{2,1,0:T(8,128)(2,1)} %get-tuple-element.14.w_ref, f32[4,4,256,256]{3,2,1,0:T(8,128)} %taper.1.taper_ref), custom_call_target="tpu_custom_call" | custom-call | tf_op jit(solution)/shard_map/update/pallas_call | solution.py:379
Async XLA Ops:
  3.2 6.5 %collective-permute-start = (f32[32,512]{1,0:T(8,128)}, f32[32,512]{1,0:T(8,128)S(1)}, u32[]{:S(2)}, u32[]{:S(2)}) collective-permute-start(f32[32,512]{1,0:T(8,128)} %get-tuple-element.10), channel_id=1, source_target_pairs={{0,8},{8,16},{16,24},{24,0},{1,9},{9,17},{17,25},{25,1},{2,10},{10... | collective-permute-start | bytes 196616 | tf_op jit(solution)/shard_map/ppermute | solution.py:328
  6.2 4.9 %collective-permute-start.1 = (f32[32,512]{1,0:T(8,128)}, f32[32,512]{1,0:T(8,128)S(1)}, u32[]{:S(2)}, u32[]{:S(2)}) collective-permute-start(f32[32,512]{1,0:T(8,128)} %get-tuple-element.11), channel_id=1, source_target_pairs={{0,24},{8,0},{16,8},{24,16},{1,25},{9,1},{17,9},{25,17},{2,26},{10... | collective-permute-start | bytes 196616 | tf_op jit(solution)/shard_map/ppermute | solution.py:329
  9.7 1.4 %copy-start.2 = (f32[32,512]{1,0:T(8,128)}, f32[32,512]{1,0:T(8,128)S(1)}, u32[]{:S(2)}) copy-start(f32[32,512]{1,0:T(8,128)S(1)} %collective-permute-done.low_ref) | copy-start | bytes 196612
  11.1 0.6 copy-start.3
  16.4 68.1 %all-to-all-start = ((f32[8,8,3072]{2,1,0:T(8,128)}), f32[8,8,3072]{2,1,0:T(8,128)S(1)}, u32[]{:S(2)}, u32[]{:S(2)}) async-start(f32[8,8,3072]{2,1,0:T(8,128)} %forecast.1), calls=%async_computation | async-start | bytes 1572864 | tf_op jit(solution)/shard_map/all_to_all | solution.py:344
  21.5 4.1 %collective-permute-start.4 = (f32[8,1024]{1,0:T(8,128)}, f32[8,1024]{1,0:T(8,128)S(1)}, u32[]{:S(2)}, u32[]{:S(2)}) collective-permute-start(f32[8,1024]{1,0:T(8,128)} %get-tuple-element.12), channel_id=1, source_target_pairs={{0,24},{8,0},{16,8},{24,16},{1,25},{9,1},{17,9},{25,17},{2,26},{10... | collective-permute-start | bytes 98312 | tf_op jit(solution)/shard_map/ppermute | solution.py:327
  23.2 4.1 %collective-permute-start.3 = (f32[8,1024]{1,0:T(8,128)}, f32[8,1024]{1,0:T(8,128)S(1)}, u32[]{:S(2)}, u32[]{:S(2)}) collective-permute-start(f32[8,1024]{1,0:T(8,128)} %get-tuple-element.12), channel_id=1, source_target_pairs={{0,16},{8,24},{16,0},{24,8},{1,17},{9,25},{17,1},{25,9},{2,18},{10... | collective-permute-start | bytes 98312 | tf_op jit(solution)/shard_map/ppermute | solution.py:327
  24.7 5.0 %collective-permute-start.2 = (f32[8,1024]{1,0:T(8,128)}, f32[8,1024]{1,0:T(8,128)S(1)}, u32[]{:S(2)}, u32[]{:S(2)}) collective-permute-start(f32[8,1024]{1,0:T(8,128)} %get-tuple-element.12), channel_id=1, source_target_pairs={{0,8},{8,16},{16,24},{24,0},{1,9},{9,17},{17,25},{25,1},{2,10},{10... | collective-permute-start | bytes 98312 | tf_op jit(solution)/shard_map/ppermute | solution.py:327
  30.5 22.4 %copy-start.1 = (f32[8,1024]{1,0:T(8,128)}, f32[8,1024]{1,0:T(8,128)S(1)}, u32[]{:S(2)}) copy-start(f32[8,1024]{1,0:T(8,128)S(1)} %add_add_fusion.refs_7_) | copy-start | bytes 98308
  30.6 6.6 %collective-permute-start.11 = (f32[8,1024]{1,0:T(8,128)S(1)}, f32[8,1024]{1,0:T(8,128)S(1)}, u32[]{:S(2)}, u32[]{:S(2)}) collective-permute-start(f32[8,1024]{1,0:T(8,128)S(1)} %add_add_fusion.refs_7_), channel_id=1, source_target_pairs={{0,7},{1,0},{2,1},{3,2},{4,3},{5,4},{6,5},{7,6},{8,15},{9,8},{10,9... | collective-permute-start | bytes 98312 | tf_op jit(solution)/shard_map/ppermute | solution.py:333
  32.7 5.3 %collective-permute-start.10 = (f32[8,1024]{1,0:T(8,128)S(1)}, f32[8,1024]{1,0:T(8,128)S(1)}, u32[]{:S(2)}, u32[]{:S(2)}) collective-permute-start(f32[8,1024]{1,0:T(8,128)S(1)} %add_add_fusion.refs_7_), channel_id=1, source_target_pairs={{0,6},{1,7},{2,0},{3,1},{4,2},{5,3},{6,4},{7,5},{8,14},{9,15},{10,... | collective-permute-start | bytes 98312 | tf_op jit(solution)/shard_map/ppermute | solution.py:333
  34.5 18.4 %collective-permute-start.9 = (f32[8,1024]{1,0:T(8,128)S(1)}, f32[8,1024]{1,0:T(8,128)S(1)}, u32[]{:S(2)}, u32[]{:S(2)}) collective-permute-start(f32[8,1024]{1,0:T(8,128)S(1)} %add_add_fusion.refs_7_), channel_id=1, source_target_pairs={{0,5},{1,6},{2,7},{3,0},{4,1},{5,2},{6,3},{7,4},{8,13},{9,14},{10,... | collective-permute-start | bytes 98312 | tf_op jit(solution)/shard_map/ppermute | solution.py:333
  34.5 18.4 %collective-permute-start.8 = (f32[8,1024]{1,0:T(8,128)S(1)}, f32[8,1024]{1,0:T(8,128)S(1)}, u32[]{:S(2)}, u32[]{:S(2)}) collective-permute-start(f32[8,1024]{1,0:T(8,128)S(1)} %add_add_fusion.refs_7_), channel_id=1, source_target_pairs={{0,4},{1,5},{2,6},{3,7},{4,0},{5,1},{6,2},{7,3},{8,12},{9,13},{10,... | collective-permute-start | bytes 98312 | tf_op jit(solution)/shard_map/ppermute | solution.py:333
  37.2 15.7 %collective-permute-start.7 = (f32[8,1024]{1,0:T(8,128)S(1)}, f32[8,1024]{1,0:T(8,128)S(1)}, u32[]{:S(2)}, u32[]{:S(2)}) collective-permute-start(f32[8,1024]{1,0:T(8,128)S(1)} %add_add_fusion.refs_7_), channel_id=1, source_target_pairs={{0,3},{1,4},{2,5},{3,6},{4,7},{5,0},{6,1},{7,2},{8,11},{9,12},{10,... | collective-permute-start | bytes 98312 | tf_op jit(solution)/shard_map/ppermute | solution.py:333
  37.2 15.8 %copy-start.4 = (f32[8,1024]{1,0:T(8,128)}, f32[8,1024]{1,0:T(8,128)S(1)}, u32[]{:S(2)}) copy-start(f32[8,1024]{1,0:T(8,128)S(1)} %collective-permute-done.11.refs_14_) | copy-start | bytes 98308
  37.2 15.7 %collective-permute-start.6 = (f32[8,1024]{1,0:T(8,128)S(1)}, f32[8,1024]{1,0:T(8,128)S(1)}, u32[]{:S(2)}, u32[]{:S(2)}) collective-permute-start(f32[8,1024]{1,0:T(8,128)S(1)} %add_add_fusion.refs_7_), channel_id=1, source_target_pairs={{0,2},{1,3},{2,4},{3,5},{4,6},{5,7},{6,0},{7,1},{8,10},{9,11},{10,... | collective-permute-start | bytes 98312 | tf_op jit(solution)/shard_map/ppermute | solution.py:333
  38.0 15.0 %copy-start.5 = (f32[8,1024]{1,0:T(8,128)}, f32[8,1024]{1,0:T(8,128)S(1)}, u32[]{:S(2)}) copy-start(f32[8,1024]{1,0:T(8,128)S(1)} %collective-permute-done.10.refs_13_) | copy-start | bytes 98308
  38.0 15.0 %collective-permute-start.5 = (f32[8,1024]{1,0:T(8,128)S(1)}, f32[8,1024]{1,0:T(8,128)S(1)}, u32[]{:S(2)}, u32[]{:S(2)}) collective-permute-start(f32[8,1024]{1,0:T(8,128)S(1)} %add_add_fusion.refs_7_), channel_id=1, source_target_pairs={{0,1},{1,2},{2,3},{3,4},{4,5},{5,6},{6,7},{7,0},{8,9},{9,10},{10,1... | collective-permute-start | bytes 98312 | tf_op jit(solution)/shard_map/ppermute | solution.py:333
  52.9 0.6 copy-start.6
  52.9 0.6 copy-start.7
  52.9 0.6 copy-start.8
  52.9 0.6 copy-start.9
  53.0 0.6 copy-start.10
  84.6 0.9 copy-start

commit v2 on v1

--- a/solution.py
+++ b/solution.py
@@ -8,9 +8,12 @@
 from jax.experimental.pallas import tpu as pltpu
 from jax.sharding import PartitionSpec as P
 
+
 COURANT = 0.3
 ROTATION = 0.1
 HALF = COURANT * 0.5
+ROUNDS = 6
+CONVERGED = 1e6
 F32 = jnp.float32
 BF16 = jnp.bfloat16
 VMEM_SPEC = pl.BlockSpec(memory_space=pltpu.VMEM)
@@ -96,8 +99,26 @@
     return (u[0], q, r, s), (first, HALF * HALF * q, HALF * HALF * h1)
 
 
-def prior_kernel(members, cells_x, slabs, batches, me_ref, owner_ref, x_ref, offset_ref,
-                 obs_ref, low_ref, high_ref, rows_ref, lanes_ref):
+def edges_kernel(members, cells_x, x_ref, low_ref, high_ref, added_ref, lanes_ref):
+    keep_lanes(lanes_ref, 0, x_ref[...])
+
+    def across(field, row):
+        return every_nth(lanes_ref, field * cells_x + row, members, 3 * cells_x)
+
+    last = cells_x - 1
+    for side, (out_ref, sign) in enumerate(((low_ref, 1.0), (high_ref, -1.0))):
+        rows = [last - i if sign > 0 else i for i in range(4)]
+        sent, added = edge_rows(
+            [across(0, i) for i in rows[:3]], [across(1, i) for i in rows],
+            [across(2, i) for i in rows[:3]], sign)
+        for i in range(4):
+            out_ref[pl.ds(i * members, members), :] = sent[i]
+        for i in range(3):
+            added_ref[pl.ds((3 * side + i) * members, members), :] = added[i]
+
+
+def prior_kernel(members, cells_x, slabs, batches, me_ref, owner_ref, x_ref, added_ref, offset_ref,
+                 obs_ref, rows_ref):
     cells_y = x_ref.shape[1]
     nobs = offset_ref.shape[1]
     zero = (jnp.zeros((1, cells_y), F32),) * 4
@@ -106,27 +127,7 @@
         start = m * 3 * cells_x
         h, u, v = (x_ref[pl.ds(start + f * cells_x, cells_x), :] for f in range(3))
         rows_ref[pl.ds(m * cells_x, cells_x), :] = wave_twice(h, u, v, zero, zero, False)
-
-    keep_lanes(lanes_ref, 0, x_ref[...])
-
-    def across(field, row):
-        return every_nth(lanes_ref, field * cells_x + row, members, 3 * cells_x)
-
-    last = cells_x - 1
-    sent, added = edge_rows(
-        [across(0, last - i) for i in range(3)], [across(1, last - i) for i in range(4)],
-        [across(2, last - i) for i in range(3)], 1.0)
-    for i in range(4):
-        low_ref[pl.ds(i * members, members), :] = sent[i]
-    for i in range(3):
-        rows_ref[pl.ds(base + i * members, members), :] = added[i]
-    sent, added = edge_rows(
-        [across(0, i) for i in range(3)], [across(1, i) for i in range(4)],
-        [across(2, i) for i in range(3)], -1.0)
-    for i in range(4):
-        high_ref[pl.ds(i * members, members), :] = sent[i]
-    for i in range(3):
-        rows_ref[pl.ds(base + (3 + i) * members, members), :] = added[i]
+    rows_ref[pl.ds(base, 6 * members), :] = added_ref[...]
 
     values = rows_ref[...]
     part0 = values.astype(BF16)
@@ -200,7 +201,6 @@
 
 def taper_kernel(slabs, cells_x, cells_y, batches, tile, groups, first_ref, owner_ref, offset_ref,
                  cutoff_ref, out_ref):
-    nobs = offset_ref.shape[1]
     for b in range(batches):
         row, column, inverse = geometry(owner_ref, offset_ref, cutoff_ref, b, slabs, cells_x, cells_y)
         row, column, inverse = column_of(row), column_of(column), column_of(inverse)
@@ -212,10 +212,42 @@
                                      float(cells_x * slabs), float(cells_y))
 
 
+def solve_members(gram, right, lowest, work_ref):
+    size = gram.shape[0]
+    top = jnp.max(jnp.sum(jnp.abs(gram), axis=1, keepdims=True), axis=0, keepdims=True)
+    top = jnp.maximum(top, 4.0 * lowest)
+    eye = jnp.where(
+        lax.broadcasted_iota(jnp.int32, (size, size), 0)
+        == lax.broadcasted_iota(jnp.int32, (size, size), 1), 1.0, 0.0)
+    alpha = 2.0 / (top + lowest)
+
+    def double(r, x, t):
+        t = 2.0 * t * t - 1.0
+        extra = 1.0 / t
+        both = mm_f32(r, jnp.concatenate([r, x], axis=1))
+        gain = 1.0 + extra
+        return gain * both[:, :size] - extra * eye, gain * (x + both[:, size:]), t
+
+    r, x, t = eye - alpha * gram, alpha * right, (top + lowest) / (top - lowest)
+    for _ in range(ROUNDS):
+        r, x, t = double(r, x, t)
+    work_ref[:, :size] = r
+    work_ref[:, size:] = x
+
+    def more(t):
+        r, x, t = double(work_ref[:, :size], work_ref[:, size:], jnp.full((1, 1), t, F32))
+        work_ref[:, :size] = r
+        work_ref[:, size:] = x
+        return t[0, 0]
+
+    lax.while_loop(lambda t: t < CONVERGED, more, t[0, 0])
+    return work_ref[:, size:]
+
+
 def chain_kernel(slabs, cells_x, cells_y, batches, parts, *refs):
     place_ref, owner_ref, offset_ref, cutoff_ref, values_ref, variance_ref, perturb_ref = refs[:7]
     part_refs = refs[7 : 7 + parts]
-    y_ref, w_ref, obs_ref, aug_ref = refs[7 + parts :]
+    y_ref, w_ref, obs_ref, work_ref = refs[7 + parts :]
     members = obs_ref.shape[0]
     nobs = offset_ref.shape[1]
     each = part_refs[0].shape[0]
@@ -226,7 +258,6 @@
            == lax.broadcasted_iota(jnp.int32, (members, members), 1))
     places = [geometry(owner_ref, offset_ref, cutoff_ref, b, slabs, cells_x, cells_y)
               for b in range(batches)]
-    sublane = lax.broadcasted_iota(jnp.int32, (8, 2 * members), 0)
     for b in range(batches):
         observed = obs_ref[:, b * nobs : (b + 1) * nobs]
         spread = observed - jnp.mean(observed, axis=0, keepdims=True)
@@ -235,25 +266,7 @@
         target = values_ref[b : b + 1, :] + jnp.sqrt(variance) * perturb_ref[b] - observed
         both = mm_f32(spread * inverse, jnp.concatenate([spread, target], axis=0), ((1,), (1,)))
         gram = both[:, :members] + jnp.where(eye, float(members - 1), 0.0)
-        aug_ref[:, :members] = gram
-        aug_ref[:, members:] = both[:, members:]
-
-        def eliminate(block, carry):
-            at = pl.ds(pl.multiple_of(block * 8, 8), 8)
-            panel = aug_ref[at, :]
-            for j in range(8):
-                line = panel[j : j + 1, :] * (1.0 / panel[j : j + 1, j : j + 1])
-                panel = jnp.where(sublane == j, line, panel - panel[:, j : j + 1] * line)
-            every = aug_ref[...]
-            for j in range(8):
-                every = every - every[:, j : j + 1] * panel[j : j + 1, :] if j == 0 else every - aug_ref[:, j : j + 1] * panel[j : j + 1, :]
-            aug_ref[...] = every
-            aug_ref[at, :] = panel
-            aug_ref[...] = pltpu.roll(aug_ref[...], 2 * members - 8, 1)
-            return carry
-
-        lax.fori_loop(0, members // 8, eliminate, 0)
-        solved = aug_ref[:, :members]
+        solved = solve_members(gram, both[:, members:], float(members - 1), work_ref)
         weights = (target - mm_f32(solved, spread, ((0,), (0,)))) * inverse
         spread_t = jnp.transpose(spread) * scale
         high, low = split2(spread_t)
@@ -306,31 +319,36 @@
     def shift(count, by):
         return [(i, (i + by) % count) for i in range(count)]
 
-    partial, low, high = pl.pallas_call(
+    def permute(array, axis, count, by):
+        return lax.ppermute(array, axis, shift(count, by))
+
+    edge = jax.ShapeDtypeStruct((4 * each, cells_y), F32)
+    low, high, added = pl.pallas_call(
+        functools.partial(edges_kernel, each, cells_x),
+        out_shape=(edge, edge, jax.ShapeDtypeStruct((6 * each, cells_y), F32)),
+        in_specs=[VMEM_SPEC],
+        out_specs=(VMEM_SPEC,) * 3,
+        scratch_shapes=[pltpu.VMEM((cells_y // 128, each * 3 * cells_x, 128), F32)],
+        name="edges",
+    )(x)
+    low = lax.ppermute(low, "slab", shift(slabs, 1))
+    high = lax.ppermute(high, "slab", shift(slabs, -1))
+
+    partial = pl.pallas_call(
         functools.partial(prior_kernel, each, cells_x, slabs, batches),
-        out_shape=(
-            jax.ShapeDtypeStruct((each, batches * nobs), F32),
-            jax.ShapeDtypeStruct((4 * each, cells_y), F32),
-            jax.ShapeDtypeStruct((4 * each, cells_y), F32),
-        ),
-        in_specs=[SMEM_SPEC, SMEM_SPEC, VMEM_SPEC, VMEM_SPEC],
-        out_specs=(VMEM_SPEC,) * 3,
-        scratch_shapes=[
-            pltpu.VMEM((each * cells_x + 6 * each, cells_y), F32),
-            pltpu.VMEM((cells_y // 128, each * 3 * cells_x, 128), F32),
-        ],
+        out_shape=jax.ShapeDtypeStruct((each, batches * nobs), F32),
+        in_specs=[SMEM_SPEC, SMEM_SPEC, VMEM_SPEC, VMEM_SPEC, VMEM_SPEC],
+        out_specs=VMEM_SPEC,
+        scratch_shapes=[pltpu.VMEM((each * cells_x + 6 * each, cells_y), F32)],
         name="prior",
-    )(slab.reshape(1), owner, x, obs_offset)
+    )(slab.reshape(1), owner, x, added, obs_offset)
 
     observed = partial
     for by in range(1, slabs):
-        observed = observed + lax.ppermute(partial, "slab", shift(slabs, by))
-    low = lax.ppermute(low, "slab", shift(slabs, 1))
-    high = lax.ppermute(high, "slab", shift(slabs, -1))
-
+        observed = observed + permute(partial, "slab", slabs, by)
     pieces = [observed]
     for by in range(1, shards):
-        pieces.append(lax.ppermute(observed, "member", shift(shards, by)))
+        pieces.append(permute(observed, "member", shards, by))
     place = lax.rem(member - jnp.arange(shards, dtype=jnp.int32) + shards, shards)
 
     outgoing = pl.pallas_call(
@@ -354,14 +372,15 @@
         groups = [[at] for at in range(0, chunk, tile)]
     first = (slab * shards + member) * chunk
     taper = pl.pallas_call(
-        functools.partial(taper_kernel, slabs, cells_x, cells_y, batches, tile, [g[0] for g in groups]),
+        functools.partial(
+            taper_kernel, slabs, cells_x, cells_y, batches, tile, [g[0] for g in groups]),
         out_shape=jax.ShapeDtypeStruct((batches, len(groups), nobs, tile), F32),
         in_specs=[SMEM_SPEC, SMEM_SPEC, VMEM_SPEC, VMEM_SPEC],
         out_specs=VMEM_SPEC,
         name="taper",
     )(first.reshape(1), owner, obs_offset, taper_cutoff)
 
-    y_all, w_all = pl.pallas_call(
+    chain = pl.pallas_call(
         functools.partial(chain_kernel, slabs, cells_x, cells_y, batches, shards),
         out_shape=(
             jax.ShapeDtypeStruct((batches, nobs, 3 * members), BF16),
@@ -374,7 +393,9 @@
             pltpu.VMEM((members, 2 * members), F32),
         ],
         name="chain",
-    )(place, owner, obs_offset, taper_cutoff, obs_values, obs_variance, perturb, *pieces)
+    )
+    y_all, w_all = chain(
+        place, owner, obs_offset, taper_cutoff, obs_values, obs_variance, perturb, *pieces)
 
     return pl.pallas_call(
         functools.partial(update_kernel, batches, tile, groups),
@@ -388,6 +409,5 @@
 def solution(mesh):
     in_specs = (P("member", "slab", None, None), P(), P(), P(), P(), P(), P())
     out_specs = P(None, ("slab", "member"))
-    return jax.shard_map(
-        on_device, mesh=mesh, in_specs=in_specs, out_specs=out_specs, check_vma=False
-    )
+
+    return jax.shard_map(on_device, mesh=mesh, in_specs=in_specs, out_specs=out_specs, check_vma=False)

time: 96.8 us -> 76.6 us (0.79)
  Pallas kernels: 54.8 us -> 37.7 us
  starting transfers between devices: 28.3 us -> 25.1 us
    pallas_call x1 -> x2, Pallas kernels: 31 us -> 13.9 us  [the longest x1 11.9 us: on_device(): chain(place, owner, obs_offset, taper_cutoff, obs_values, obs_variance, p...]
    ppermute x10, starting transfers between devices: 19.3 us -> 16.1 us  [permute(): return lax.ppermute(array, axis, shift(count, by))]
  transfers between devices with their start and end apart: 13 -> 13, of which waited for: 5 -> 5; matrix products, arithmetic and copies ran while one was open for 1% -> 2% of each run, Pallas kernels for 38% -> 28%
where the time goes in v2:
time: 76.6 us; the launch traced here: 75.4 us
  Pallas kernels  37.7 us (49%)
  starting transfers between devices  25.1 us (33%)
  waiting for transfers between devices  8.99 us (12%)
  local copies, waits for them, and re-layouts  2.11 us (3%)
  other arithmetic  1.35 us (2%)
    ppermute x10, starting transfers between devices, permute(): return lax.ppermute(array, axis, shift(count, by))  16.1 us
    pallas_call x1, Pallas kernels, on_device(): chain(place, owner, obs_offset, taper_cutoff, obs_values, obs_variance, p...  11.9 us
    pallas_call x1, Pallas kernels, on_device(): pl.pallas_call(functools.partial(update_kernel, batches, tile, groups), o...  10.2 us
    pallas_call x1, Pallas kernels, on_device(): pl.pallas_call(functools.partial(taper_kernel, slabs, cells_x, cells_y, b...  5.7 us
    all_to_all x1, starting transfers between devices, on_device(): state = lax.all_to_all(outgoing, 'member', 0, 0).reshape(members, chunk)  5.04 us
    ppermute x10, waiting for transfers between devices, permute(): return lax.ppermute(array, axis, shift(count, by))  5.04 us
    pallas_call x1, Pallas kernels, on_device(): pl.pallas_call(functools.partial(forecast_kernel, each, cells_x), out_sha...  4.69 us
    pallas_call x1, Pallas kernels, on_device(): pl.pallas_call(functools.partial(prior_kernel, each, cells_x, slabs, batc...  3.18 us
  transfers between devices with their start and end apart: 13, of which 5 were waited for; matrix products, arithmetic and copies ran while one was open for 2% of the time, Pallas kernels for 28%

profile of v2, /device:TPU:0, one launch (start us, length us, event | category | flops | bytes accessed | tf_op | source)
XLA Modules:
  0.0 75.4 jit_solution(5397397976182409156)
XLA Ops:
  0.0 2.0 %edges.1 = (f32[32,512]{1,0:T(8,128)}, f32[32,512]{1,0:T(8,128)}, f32[48,512]{1,0:T(8,128)}) custom-call(f32[384,512]{1,0:T(8,128)} %bitcast.7), custom_call_target="tpu_custom_call" | custom-call | tf_op jit(solution)/shard_map/edges/pallas_call | solution.py:326
  2.0 3.0 %collective-permute-start = (f32[32,512]{1,0:T(8,128)}, f32[32,512]{1,0:T(8,128)S(1)}, u32[]{:S(2)}, u32[]{:S(2)}) collective-permute-start(f32[32,512]{1,0:T(8,128)} %get-tuple-element.10), channel_id=1, source_target_pairs={{0,8},{8,16},{16,24},{24,0},{1,9},{9,17},{17,25},{25,1},{2,10},{10... | collective-permute-start | bytes 196616 | tf_op jit(solution)/shard_map/ppermute | solution.py:334
  5.0 1.0 %collective-permute-start.1 = (f32[32,512]{1,0:T(8,128)}, f32[32,512]{1,0:T(8,128)S(1)}, u32[]{:S(2)}, u32[]{:S(2)}) collective-permute-start(f32[32,512]{1,0:T(8,128)} %get-tuple-element.11), channel_id=1, source_target_pairs={{0,24},{8,0},{16,8},{24,16},{1,25},{9,1},{17,9},{25,17},{2,26},{10... | collective-permute-start | bytes 196616 | tf_op jit(solution)/shard_map/ppermute | solution.py:335
  5.9 2.5 %collective-permute-done.low_ref = f32[32,512]{1,0:T(8,128)S(1)} collective-permute-done((f32[32,512]{1,0:T(8,128)}, f32[32,512]{1,0:T(8,128)S(1)}, u32[]{:S(2)}, u32[]{:S(2)}) %collective-permute-start) | collective-permute-done | bytes 65568 | tf_op jit(solution)/shard_map/ppermute | solution.py:334
  8.5 0.0 copy-start.2
  8.5 1.4 %collective-permute-done.1.high_ref = f32[32,512]{1,0:T(8,128)S(1)} collective-permute-done((f32[32,512]{1,0:T(8,128)}, f32[32,512]{1,0:T(8,128)S(1)}, u32[]{:S(2)}, u32[]{:S(2)}) %collective-permute-start.1) | collective-permute-done | bytes 65568 | tf_op jit(solution)/shard_map/ppermute | solution.py:335
  9.9 0.0 copy-done.2
  9.9 0.0 copy-start.3
  9.9 0.6 copy-done.3
  10.5 4.7 %forecast.1 = f32[8,8,3072]{2,1,0:T(8,128)} custom-call(f32[384,512]{1,0:T(8,128)} %bitcast.8, f32[32,512]{1,0:T(8,128)} %copy-done.2, f32[32,512]{1,0:T(8,128)} %copy-done.3), custom_call_target="tpu_custom_call" | custom-call | tf_op jit(solution)/shard_map/forecast/pallas_call | solution.py:354
  15.2 5.0 %all-to-all-start = ((f32[8,8,3072]{2,1,0:T(8,128)}), f32[8,8,3072]{2,1,0:T(8,128)S(1)}, u32[]{:S(2)}, u32[]{:S(2)}) async-start(f32[8,8,3072]{2,1,0:T(8,128)} %forecast.1), calls=%async_computation | async-start | bytes 1572864 | tf_op jit(solution)/shard_map/all_to_all | solution.py:362
  20.3 3.2 %prior.1 = f32[8,1024]{1,0:T(8,128)} custom-call(s32[1]{0:T(128)} %bitcast.5.me_ref, s32[4]{0:T(128)} %owner_ref.3, f32[384,512]{1,0:T(8,128)} %bitcast.9, f32[48,512]{1,0:T(8,128)} %get-tuple-element.12.added_ref, s32[4,256]{1,0:T(4,128)} %offset_ref.3), custom_call_target="tpu_custom_call" | custom-call | tf_op jit(solution)/shard_map/prior/pallas_call | solution.py:337
  23.4 1.7 %collective-permute-start.4 = (f32[8,1024]{1,0:T(8,128)}, f32[8,1024]{1,0:T(8,128)S(1)}, u32[]{:S(2)}, u32[]{:S(2)}) collective-permute-start(f32[8,1024]{1,0:T(8,128)} %prior.1), channel_id=1, source_target_pairs={{0,24},{8,0},{16,8},{24,16},{1,25},{9,1},{17,9},{25,17},{2,26},{10... | collective-permute-start | bytes 98312 | tf_op jit(solution)/shard_map/ppermute | solution.py:323
  25.2 1.5 %collective-permute-start.3 = (f32[8,1024]{1,0:T(8,128)}, f32[8,1024]{1,0:T(8,128)S(1)}, u32[]{:S(2)}, u32[]{:S(2)}) collective-permute-start(f32[8,1024]{1,0:T(8,128)} %prior.1), channel_id=1, source_target_pairs={{0,16},{8,24},{16,0},{24,8},{1,17},{9,25},{17,1},{25,9},{2,18},{10... | collective-permute-start | bytes 98312 | tf_op jit(solution)/shard_map/ppermute | solution.py:323
  26.7 0.0 collective-permute-start.2
  26.7 0.9 %collective-permute-done.4 = f32[8,1024]{1,0:T(8,128)S(1)} collective-permute-done((f32[8,1024]{1,0:T(8,128)}, f32[8,1024]{1,0:T(8,128)S(1)}, u32[]{:S(2)}, u32[]{:S(2)}) %collective-permute-start.4) | collective-permute-done | bytes 32800 | tf_op jit(solution)/shard_map/ppermute | solution.py:323
  27.6 1.7 %collective-permute-done.3 = f32[8,1024]{1,0:T(8,128)S(1)} collective-permute-done((f32[8,1024]{1,0:T(8,128)}, f32[8,1024]{1,0:T(8,128)S(1)}, u32[]{:S(2)}, u32[]{:S(2)}) %collective-permute-start.3) | collective-permute-done | bytes 32800 | tf_op jit(solution)/shard_map/ppermute | solution.py:323
  29.3 2.4 %collective-permute-done.2 = f32[8,1024]{1,0:T(8,128)S(1)} collective-permute-done((f32[8,1024]{1,0:T(8,128)}, f32[8,1024]{1,0:T(8,128)S(1)}, u32[]{:S(2)}, u32[]{:S(2)}) %collective-permute-start.2) | collective-permute-done | bytes 32800 | tf_op jit(solution)/shard_map/ppermute | solution.py:323
  31.7 0.8 %add_add_fusion.refs_7_ = f32[8,1024]{1,0:T(8,128)S(1)} fusion(f32[8,1024]{1,0:T(8,128)S(1)} %collective-permute-done.4, f32[8,1024]{1,0:T(8,128)S(1)} %collective-permute-done.3, f32[8,1024]{1,0:T(8,128)} %prior.1, f32[8,1024]{1,0:T(8,128)S(1)} %collective-permute-done.2), kind=kLoop, calls=%fused_computation | loop fusion | flops 24576 | bytes 163840 | tf_op jit(solution)/shard_map/add | solution.py:348
  32.5 0.0 copy-start.1
  32.5 2.0 %collective-permute-start.11 = (f32[8,1024]{1,0:T(8,128)S(1)}, f32[8,1024]{1,0:T(8,128)S(1)}, u32[]{:S(2)}, u32[]{:S(2)}) collective-permute-start(f32[8,1024]{1,0:T(8,128)S(1)} %add_add_fusion.refs_7_), channel_id=1, source_target_pairs={{0,7},{1,0},{2,1},{3,2},{4,3},{5,4},{6,5},{7,6},{8,15},{9,8},{10,9... | collective-permute-start | bytes 98312 | tf_op jit(solution)/shard_map/ppermute | solution.py:323
  34.5 2.0 %collective-permute-start.10 = (f32[8,1024]{1,0:T(8,128)S(1)}, f32[8,1024]{1,0:T(8,128)S(1)}, u32[]{:S(2)}, u32[]{:S(2)}) collective-permute-start(f32[8,1024]{1,0:T(8,128)S(1)} %add_add_fusion.refs_7_), channel_id=1, source_target_pairs={{0,6},{1,7},{2,0},{3,1},{4,2},{5,3},{6,4},{7,5},{8,14},{9,15},{10,... | collective-permute-start | bytes 98312 | tf_op jit(solution)/shard_map/ppermute | solution.py:323
  36.4 0.0 collective-permute-start.9
  36.4 2.7 %collective-permute-start.8 = (f32[8,1024]{1,0:T(8,128)S(1)}, f32[8,1024]{1,0:T(8,128)S(1)}, u32[]{:S(2)}, u32[]{:S(2)}) collective-permute-start(f32[8,1024]{1,0:T(8,128)S(1)} %add_add_fusion.refs_7_), channel_id=1, source_target_pairs={{0,4},{1,5},{2,6},{3,7},{4,0},{5,1},{6,2},{7,3},{8,12},{9,13},{10,... | collective-permute-start | bytes 98312 | tf_op jit(solution)/shard_map/ppermute | solution.py:323
  39.1 0.0 collective-permute-start.7
  39.1 0.0 collective-permute-done.11.refs_14_
  39.1 0.0 copy-start.4
  39.1 0.8 %collective-permute-start.6 = (f32[8,1024]{1,0:T(8,128)S(1)}, f32[8,1024]{1,0:T(8,128)S(1)}, u32[]{:S(2)}, u32[]{:S(2)}) collective-permute-start(f32[8,1024]{1,0:T(8,128)S(1)} %add_add_fusion.refs_7_), channel_id=1, source_target_pairs={{0,2},{1,3},{2,4},{3,5},{4,6},{5,7},{6,0},{7,1},{8,10},{9,11},{10,... | collective-permute-start | bytes 98312 | tf_op jit(solution)/shard_map/ppermute | solution.py:323
  39.9 0.0 collective-permute-done.10.refs_13_
  39.9 0.0 copy-start.5
  39.9 5.5 %collective-permute-start.5 = (f32[8,1024]{1,0:T(8,128)S(1)}, f32[8,1024]{1,0:T(8,128)S(1)}, u32[]{:S(2)}, u32[]{:S(2)}) collective-permute-start(f32[8,1024]{1,0:T(8,128)S(1)} %add_add_fusion.refs_7_), channel_id=1, source_target_pairs={{0,1},{1,2},{2,3},{3,4},{4,5},{5,6},{6,7},{7,0},{8,9},{9,10},{10,1... | collective-permute-start | bytes 98312 | tf_op jit(solution)/shard_map/ppermute | solution.py:323
  45.4 0.6 compare_select_fusion.refs_0_
  46.0 5.7 %taper.1.taper_ref = f32[4,4,256,256]{3,2,1,0:T(8,128)} custom-call(s32[1]{0:T(128)} %bitcast.6.first_ref, s32[4]{0:T(128)} %owner_ref.3, s32[4,256]{1,0:T(4,128)} %offset_ref.3, s32[4,256]{1,0:T(4,128)} %cutoff_ref.1), custom_call_target="tpu_custom_call" | custom-call | tf_op jit(solution)/shard_map/taper/pallas_call | solution.py:374
  51.7 0.0 collective-permute-done.9.refs_12_
  51.7 0.0 copy-start.6
  51.7 0.0 collective-permute-done.8.refs_11_
  51.7 0.0 copy-start.7
  51.7 0.0 collective-permute-done.7.refs_10_
  51.7 0.0 copy-start.8
  51.7 0.0 collective-permute-done.6.refs_9_
  51.7 0.0 copy-start.9
  51.7 0.0 collective-permute-done.5.refs_8_
  51.7 0.0 copy-start.10
  51.8 0.0 copy-done.1
  51.8 0.0 copy-done.4
  51.8 0.0 copy-done.5
  51.8 0.5 copy-done.6
  52.3 0.0 copy-done.7
  52.3 0.0 copy-done.8
  52.3 0.0 copy-done.9
  52.3 0.0 copy-done.10
  52.4 11.9 %chain.1 = (bf16[4,256,192]{2,1,0:T(8,128)(2,1)}, bf16[4,128,256]{2,1,0:T(8,128)(2,1)}) custom-call(s32[8]{0:T(128)} %compare_select_fusion.refs_0_, s32[4]{0:T(128)} %owner_ref.3, s32[4,256]{1,0:T(4,128)} %offset_ref.3, s32[4,256]{1,0:T(4,128)} %cutoff_ref.1, f32[4,256]{1,0:T(4,128)} %refs_4_.1, f32[4,256]{1,0:T(4,128)} %refs_5_.1, f32[4,64,256]{2,1,0:T(8,128)} %bitcast.11, ...), custom_call_target="tpu_custom_call" | custom-call | tf_op jit(solution)/shard_map/chain/pallas_call | solution.py:397
  64.3 0.0 all-to-all-done
  64.3 0.0 copy-start
  64.3 0.9 %copy-done = f32[8,8,3072]{2,1,0:T(8,128)} copy-done((f32[8,8,3072]{2,1,0:T(8,128)}, f32[8,8,3072]{2,1,0:T(8,128)S(1)}, u32[]{:S(2)}) %copy-start) | copy-done | bytes 786456
  65.2 10.2 %update.1 = f32[64,3072]{1,0:T(8,128)} custom-call(f32[64,3072]{1,0:T(8,128)} %bitcast.10, bf16[4,256,192]{2,1,0:T(8,128)(2,1)} %get-tuple-element.13.y_ref, bf16[4,128,256]{2,1,0:T(8,128)(2,1)} %get-tuple-element.14.w_ref, f32[4,4,256,256]{3,2,1,0:T(8,128)} %taper.1.taper_ref), custom_call_target="tpu_custom_call" | custom-call | tf_op jit(solution)/shard_map/update/pallas_call | solution.py:400
Async XLA Ops:
  2.0 6.5 %collective-permute-start = (f32[32,512]{1,0:T(8,128)}, f32[32,512]{1,0:T(8,128)S(1)}, u32[]{:S(2)}, u32[]{:S(2)}) collective-permute-start(f32[32,512]{1,0:T(8,128)} %get-tuple-element.10), channel_id=1, source_target_pairs={{0,8},{8,16},{16,24},{24,0},{1,9},{9,17},{17,25},{25,1},{2,10},{10... | collective-permute-start | bytes 196616 | tf_op jit(solution)/shard_map/ppermute | solution.py:334
  5.0 4.9 %collective-permute-start.1 = (f32[32,512]{1,0:T(8,128)}, f32[32,512]{1,0:T(8,128)S(1)}, u32[]{:S(2)}, u32[]{:S(2)}) collective-permute-start(f32[32,512]{1,0:T(8,128)} %get-tuple-element.11), channel_id=1, source_target_pairs={{0,24},{8,0},{16,8},{24,16},{1,25},{9,1},{17,9},{25,17},{2,26},{10... | collective-permute-start | bytes 196616 | tf_op jit(solution)/shard_map/ppermute | solution.py:335
  8.5 1.4 %copy-start.2 = (f32[32,512]{1,0:T(8,128)}, f32[32,512]{1,0:T(8,128)S(1)}, u32[]{:S(2)}) copy-start(f32[32,512]{1,0:T(8,128)S(1)} %collective-permute-done.low_ref) | copy-start | bytes 196612
  9.9 0.6 copy-start.3
  15.2 49.1 %all-to-all-start = ((f32[8,8,3072]{2,1,0:T(8,128)}), f32[8,8,3072]{2,1,0:T(8,128)S(1)}, u32[]{:S(2)}, u32[]{:S(2)}) async-start(f32[8,8,3072]{2,1,0:T(8,128)} %forecast.1), calls=%async_computation | async-start | bytes 1572864 | tf_op jit(solution)/shard_map/all_to_all | solution.py:362
  23.4 4.1 %collective-permute-start.4 = (f32[8,1024]{1,0:T(8,128)}, f32[8,1024]{1,0:T(8,128)S(1)}, u32[]{:S(2)}, u32[]{:S(2)}) collective-permute-start(f32[8,1024]{1,0:T(8,128)} %prior.1), channel_id=1, source_target_pairs={{0,24},{8,0},{16,8},{24,16},{1,25},{9,1},{17,9},{25,17},{2,26},{10... | collective-permute-start | bytes 98312 | tf_op jit(solution)/shard_map/ppermute | solution.py:323
  25.2 4.1 %collective-permute-start.3 = (f32[8,1024]{1,0:T(8,128)}, f32[8,1024]{1,0:T(8,128)S(1)}, u32[]{:S(2)}, u32[]{:S(2)}) collective-permute-start(f32[8,1024]{1,0:T(8,128)} %prior.1), channel_id=1, source_target_pairs={{0,16},{8,24},{16,0},{24,8},{1,17},{9,25},{17,1},{25,9},{2,18},{10... | collective-permute-start | bytes 98312 | tf_op jit(solution)/shard_map/ppermute | solution.py:323
  26.7 5.0 %collective-permute-start.2 = (f32[8,1024]{1,0:T(8,128)}, f32[8,1024]{1,0:T(8,128)S(1)}, u32[]{:S(2)}, u32[]{:S(2)}) collective-permute-start(f32[8,1024]{1,0:T(8,128)} %prior.1), channel_id=1, source_target_pairs={{0,8},{8,16},{16,24},{24,0},{1,9},{9,17},{17,25},{25,1},{2,10},{10... | collective-permute-start | bytes 98312 | tf_op jit(solution)/shard_map/ppermute | solution.py:323
  32.5 19.3 %copy-start.1 = (f32[8,1024]{1,0:T(8,128)}, f32[8,1024]{1,0:T(8,128)S(1)}, u32[]{:S(2)}) copy-start(f32[8,1024]{1,0:T(8,128)S(1)} %add_add_fusion.refs_7_) | copy-start | bytes 98308
  32.5 6.6 %collective-permute-start.11 = (f32[8,1024]{1,0:T(8,128)S(1)}, f32[8,1024]{1,0:T(8,128)S(1)}, u32[]{:S(2)}, u32[]{:S(2)}) collective-permute-start(f32[8,1024]{1,0:T(8,128)S(1)} %add_add_fusion.refs_7_), channel_id=1, source_target_pairs={{0,7},{1,0},{2,1},{3,2},{4,3},{5,4},{6,5},{7,6},{8,15},{9,8},{10,9... | collective-permute-start | bytes 98312 | tf_op jit(solution)/shard_map/ppermute | solution.py:323
  34.5 5.5 %collective-permute-start.10 = (f32[8,1024]{1,0:T(8,128)S(1)}, f32[8,1024]{1,0:T(8,128)S(1)}, u32[]{:S(2)}, u32[]{:S(2)}) collective-permute-start(f32[8,1024]{1,0:T(8,128)S(1)} %add_add_fusion.refs_7_), channel_id=1, source_target_pairs={{0,6},{1,7},{2,0},{3,1},{4,2},{5,3},{6,4},{7,5},{8,14},{9,15},{10,... | collective-permute-start | bytes 98312 | tf_op jit(solution)/shard_map/ppermute | solution.py:323
  36.4 15.2 %collective-permute-start.9 = (f32[8,1024]{1,0:T(8,128)S(1)}, f32[8,1024]{1,0:T(8,128)S(1)}, u32[]{:S(2)}, u32[]{:S(2)}) collective-permute-start(f32[8,1024]{1,0:T(8,128)S(1)} %add_add_fusion.refs_7_), channel_id=1, source_target_pairs={{0,5},{1,6},{2,7},{3,0},{4,1},{5,2},{6,3},{7,4},{8,13},{9,14},{10,... | collective-permute-start | bytes 98312 | tf_op jit(solution)/shard_map/ppermute | solution.py:323
  36.4 15.2 %collective-permute-start.8 = (f32[8,1024]{1,0:T(8,128)S(1)}, f32[8,1024]{1,0:T(8,128)S(1)}, u32[]{:S(2)}, u32[]{:S(2)}) collective-permute-start(f32[8,1024]{1,0:T(8,128)S(1)} %add_add_fusion.refs_7_), channel_id=1, source_target_pairs={{0,4},{1,5},{2,6},{3,7},{4,0},{5,1},{6,2},{7,3},{8,12},{9,13},{10,... | collective-permute-start | bytes 98312 | tf_op jit(solution)/shard_map/ppermute | solution.py:323
  39.1 12.6 %collective-permute-start.7 = (f32[8,1024]{1,0:T(8,128)S(1)}, f32[8,1024]{1,0:T(8,128)S(1)}, u32[]{:S(2)}, u32[]{:S(2)}) collective-permute-start(f32[8,1024]{1,0:T(8,128)S(1)} %add_add_fusion.refs_7_), channel_id=1, source_target_pairs={{0,3},{1,4},{2,5},{3,6},{4,7},{5,0},{6,1},{7,2},{8,11},{9,12},{10,... | collective-permute-start | bytes 98312 | tf_op jit(solution)/shard_map/ppermute | solution.py:323
  39.1 12.6 %copy-start.4 = (f32[8,1024]{1,0:T(8,128)}, f32[8,1024]{1,0:T(8,128)S(1)}, u32[]{:S(2)}) copy-start(f32[8,1024]{1,0:T(8,128)S(1)} %collective-permute-done.11.refs_14_) | copy-start | bytes 98308
  39.1 12.6 %collective-permute-start.6 = (f32[8,1024]{1,0:T(8,128)S(1)}, f32[8,1024]{1,0:T(8,128)S(1)}, u32[]{:S(2)}, u32[]{:S(2)}) collective-permute-start(f32[8,1024]{1,0:T(8,128)S(1)} %add_add_fusion.refs_7_), channel_id=1, source_target_pairs={{0,2},{1,3},{2,4},{3,5},{4,6},{5,7},{6,0},{7,1},{8,10},{9,11},{10,... | collective-permute-start | bytes 98312 | tf_op jit(solution)/shard_map/ppermute | solution.py:323
  39.9 11.8 %copy-start.5 = (f32[8,1024]{1,0:T(8,128)}, f32[8,1024]{1,0:T(8,128)S(1)}, u32[]{:S(2)}) copy-start(f32[8,1024]{1,0:T(8,128)S(1)} %collective-permute-done.10.refs_13_) | copy-start | bytes 98308
  39.9 11.8 %collective-permute-start.5 = (f32[8,1024]{1,0:T(8,128)S(1)}, f32[8,1024]{1,0:T(8,128)S(1)}, u32[]{:S(2)}, u32[]{:S(2)}) collective-permute-start(f32[8,1024]{1,0:T(8,128)S(1)} %add_add_fusion.refs_7_), channel_id=1, source_target_pairs={{0,1},{1,2},{2,3},{3,4},{4,5},{5,6},{6,7},{7,0},{8,9},{9,10},{10,1... | collective-permute-start | bytes 98312 | tf_op jit(solution)/shard_map/ppermute | solution.py:323
  51.7 0.6 copy-start.6
  51.7 0.6 copy-start.7
  51.7 0.6 copy-start.8
  51.7 0.6 copy-start.9
  51.7 0.6 copy-start.10
  64.3 0.9 %copy-start = (f32[8,8,3072]{2,1,0:T(8,128)}, f32[8,8,3072]{2,1,0:T(8,128)S(1)}, u32[]{:S(2)}) copy-start(f32[8,8,3072]{2,1,0:T(8,128)S(1)} %all-to-all-done) | copy-start | bytes 2359300

commit v3 on v2

v3 whole, which is shorter than its diff:
```python
import functools
import math

import jax
import jax.numpy as jnp
from jax import lax
from jax.experimental import pallas as pl
from jax.experimental.pallas import tpu as pltpu
from jax.sharding import PartitionSpec as P


COURANT = 0.3
ROTATION = 0.1
HALF = COURANT * 0.5
ROUNDS = 6
TINY = 1e-30
CONVERGED = 1e6
F32 = jnp.float32
BF16 = jnp.bfloat16
VMEM_SPEC = pl.BlockSpec(memory_space=pltpu.VMEM)
ANY_SPEC = pl.BlockSpec(memory_space=pl.ANY)
SMEM_SPEC = pl.BlockSpec(memory_space=pltpu.SMEM)


def d_y(field, scale=1.0):
    width = field.shape[-1]
    axis = field.ndim - 1
    return (pltpu.roll(field, width - 1, axis) - pltpu.roll(field, 1, axis)) * (0.5 * scale)


def split2(x):
    high = x.astype(BF16)
    return high, (x - high.astype(F32)).astype(BF16)


def mm(a, b):
    return lax.dot_general(a, b, (((1,), (0,)), ((), ())), preferred_element_type=F32)


def mm_f32(a, b, dims=((1,), (0,))):
    return lax.dot_general(
        a, b, (dims, ((), ())), precision=lax.Precision.HIGHEST, preferred_element_type=F32
    )


def keep_lanes(ref, start, value):
    rows, width = value.shape
    for c in range(width // 128):
        ref[c, start : start + rows, :] = value[:, c * 128 : (c + 1) * 128]


def every_nth(ref, start, count, stride):
    return jnp.concatenate(
        [ref[c, pl.ds(start, count, stride=stride), :] for c in range(ref.shape[0])], axis=1)


def row_up(field, edge, index):
    rows = field.shape[0]
    return jnp.where(index == rows - 1, edge, pltpu.roll(field, rows - 1, 0))


def row_down(field, edge, index):
    return jnp.where(index == 0, edge, pltpu.roll(field, 1, 0))


def wave_heights(h, u, v):
    rows = h.shape[0]
    index = lax.broadcasted_iota(jnp.int32, h.shape, 0)
    h1 = h - HALF * (row_up(u, 0.0, index) - row_down(u, 0.0, index)) - d_y(v, COURANT)
    below, above = -HALF * u[0:1], HALF * u[rows - 1 : rows]
    u1 = u - HALF * (row_up(h1, above, index) - row_down(h1, below, index)) + ROTATION * v
    v1 = v - d_y(h1, COURANT) - ROTATION * u
    below, above = -HALF * h1[0:1], HALF * h1[rows - 1 : rows]
    h2 = h1 - HALF * (row_up(u1, above, index) - row_down(u1, below, index)) - d_y(v1, COURANT)
    return h2, u1, v1


def edge_rows(h, u, v, sign):
    a = sign * HALF
    dv0 = COURANT * d_y(v[0])
    q = h[0] + a * u[1] - dv0
    h1_1 = h[1] - a * (u[0] - u[2]) - COURANT * d_y(v[1])
    r = u[0] + a * h1_1 + ROTATION * v[0]
    h1_2 = h[2] - a * (u[1] - u[3]) - COURANT * d_y(v[2])
    p = u[1] + a * h1_2 + ROTATION * v[1]
    s = a * p - dv0 + COURANT * ROTATION * d_y(u[0])
    h1 = a * u[0]
    first = (1.0 - 2.0 * HALF * HALF) * h1 + a * r + COURANT * COURANT * d_y(d_y(h1))
    return (u[0], q, r, s), (first, HALF * HALF * q, HALF * HALF * h1)


def prior_kernel(members, cells_x, slabs, batches, me_ref, owner_ref, x_ref, offset_ref,
                 obs_ref, next_ref, prev_ref, mid_ref, rim_ref, rows_ref, lanes_ref):
    cells_y = x_ref.shape[1]
    nobs = offset_ref.shape[1]
    base = members * cells_x
    for m in range(members):
        start = m * 3 * cells_x
        fields = [x_ref[pl.ds(start + f * cells_x, cells_x), :] for f in range(3)]
        after = wave_heights(*fields)
        rows_ref[pl.ds(m * cells_x, cells_x), :] = after[0]
        for f in range(3):
            keep_lanes(lanes_ref, start + f * cells_x, fields[f])
            keep_lanes(mid_ref, start + f * cells_x, after[f])

    def across(field, row):
        return every_nth(lanes_ref, field * cells_x + row, members, 3 * cells_x)

    last = cells_x - 1
    for side, (out_ref, sign) in enumerate(((next_ref, 1.0), (prev_ref, -1.0))):
        rows = [last - i if sign > 0 else i for i in range(4)]
        sent, added = edge_rows(
            [across(0, i) for i in rows[:3]], [across(1, i) for i in rows],
            [across(2, i) for i in rows[:3]], sign)
        for i in range(4):
            out_ref[pl.ds(i * members, members), :] = sent[i]
        for i in range(3):
            rows_ref[pl.ds(base + (3 * side + i) * members, members), :] = added[i]
        rim_ref[pl.ds((1 - side) * members, members), :] = sent[0]

    values = rows_ref[...]
    part0 = values.astype(BF16)
    rest = values - part0.astype(F32)
    part1 = rest.astype(BF16)
    part2 = (rest - part1.astype(F32)).astype(BF16)
    me = me_ref[0]
    total = cells_x * slabs
    for b in range(batches):
        offset = offset_ref[b : b + 1, :]
        column = lax.rem(offset, cells_y)
        row = lax.div(offset, cells_y)
        relative = row + lax.rem(owner_ref[b % slabs] - me + slabs, slabs) * cells_x
        pick = jnp.where(
            lax.broadcasted_iota(jnp.int32, (cells_y, nobs), 0) == column, 1.0, 0.0).astype(BF16)
        found = mm(part0, pick) + (mm(part1, pick) + mm(part2, pick))
        inside = lax.broadcasted_iota(jnp.int32, (cells_x, nobs), 0) == relative
        edges = jnp.zeros((members, nobs), F32)
        for i in range(3):
            piece = found[base + i * members : base + (i + 1) * members]
            edges += jnp.where(relative == cells_x + i, piece, 0.0)
            piece = found[base + (3 + i) * members : base + (4 + i) * members]
            edges += jnp.where(relative == total - 1 - i, piece, 0.0)
        own = [
            jnp.sum(jnp.where(inside, found[m * cells_x : (m + 1) * cells_x], 0.0),
                    axis=0, keepdims=True)
            for m in range(members)
        ]
        whole = jnp.concatenate(own, axis=0) + edges
        at = b * nobs
        place = (pl.ds(at // cells_y * members, members), slice(at % cells_y, at % cells_y + nobs))
        obs_ref[place] = whole
        for out_ref in (next_ref, prev_ref):
            out_ref[pl.ds(4 * members + at // cells_y * members, members), place[1]] = whole


def spot(chunk, cells_y, row, field, column):
    return divmod((row * 3 + field) * cells_y + column, chunk)


def forecast_kernel(members, cells_x, mid_ref, rim_ref, out_ref, rows_ref):
    cells_y = rim_ref.shape[1]
    chunk = out_ref.shape[2]
    piece = math.gcd(chunk, cells_y)
    tiles = range(cells_y // 128)
    index = lax.broadcasted_iota(jnp.int32, (cells_x, cells_y), 0)
    for m in range(members):
        start = m * 3 * cells_x
        h2, u1, v1 = (
            jnp.concatenate([mid_ref[c, start + f * cells_x : start + (f + 1) * cells_x, :] for c in tiles], axis=1)
            for f in range(3))
        u2 = u1 - HALF * (row_up(h2, 0.0, index) - row_down(h2, 0.0, index)) + ROTATION * v1
        v2 = v1 - d_y(h2, COURANT) - ROTATION * u1
        keep_lanes(rows_ref, m * 2 * cells_x, u2)
        keep_lanes(rows_ref, (m * 2 + 1) * cells_x, v2)

    def rim_height(side, sign):
        u = rim_ref[pl.ds(side * members, members), :]
        u1 = every_nth(mid_ref, cells_x + (cells_x - 1) * side, members, 3 * cells_x)
        return sign * HALF * ((1.0 - HALF * HALF) * u + COURANT * COURANT * d_y(d_y(u)) + u1)

    outside = {(0, 1): HALF * rim_height(0, -1.0), (cells_x - 1, 1): -HALF * rim_height(1, 1.0)}
    for r in range(cells_x):
        for f in range(3):
            if f == 0:
                line = every_nth(mid_ref, r, members, 3 * cells_x)
            else:
                line = every_nth(rows_ref, (f - 1) * cells_x + r, members, 2 * cells_x)
            if (r, f) in outside:
                line = line + outside[r, f]
            for c in range(0, cells_y, piece):
                dest, lane = spot(chunk, cells_y, r, f, c)
                out_ref[dest, :, lane : lane + piece] = line[:, c : c + piece]


def edge_forecast(message, members, sign):
    a = sign * HALF
    u, q, r, s = (message[i * members : (i + 1) * members] for i in range(4))
    square = COURANT * COURANT
    h1 = a * u
    u1_0, u1_1 = a * q, a * h1
    v1 = -d_y(h1, COURANT)
    h2_0 = (1.0 - 2.0 * a * a) * h1 + a * r + square * d_y(d_y(h1))
    h2_1, h2_2 = a * u1_0, a * u1_1
    h2_edge = (1.0 - 2.0 * a * a) * q + square * d_y(d_y(q)) + s
    return {
        (0, 0): h2_0, (1, 0): h2_1, (2, 0): h2_2,
        (0, 1): u1_0 - a * (h2_1 - h2_edge) + ROTATION * v1,
        (1, 1): u1_1 - a * (h2_2 - h2_0), (2, 1): a * h2_1, (3, 1): a * h2_2,
        (0, 2): v1 - COURANT * d_y(h2_0) - ROTATION * u1_0,
        (1, 2): -COURANT * d_y(h2_1) - ROTATION * u1_1, (2, 2): -COURANT * d_y(h2_2),
    }


def correct_kernel(members, cells_x, others, *refs):
    low_ref, high_ref, partial_ref = refs[:3]
    other_refs, in_ref = refs[3 : 3 + others], refs[3 + others]
    out_ref, sum_ref, message_ref, obs_ref, block_ref, in_sems, out_sems = refs[4 + others :]
    cells_y = sum_ref.shape[1]
    shards, _, chunk = in_ref.shape
    touched = block_ref.shape[1]
    piece = math.gcd(chunk, cells_y)
    spans = [pl.ds(0, touched), pl.ds(shards - touched, touched)]
    moves = [(low_ref, message_ref.at[0]), (high_ref, message_ref.at[1]), (partial_ref, obs_ref.at[0])]
    moves += [(ref, obs_ref.at[1 + i]) for i, ref in enumerate(other_refs)]
    moves += [(in_ref.at[spans[i]], block_ref.at[i]) for i in range(2)]
    copies = [pltpu.make_async_copy(a, b, in_sems.at[i]) for i, (a, b) in enumerate(moves)]
    for copy in copies:
        copy.start()
    for copy in copies:
        copy.wait()
    total = message_ref[0, 4 * members :, :] + message_ref[1, 4 * members :, :]
    for i in range(1 + others):
        total = total + obs_ref[i]
    sum_ref[...] = total
    written = []
    for side, sign in ((0, 1.0), (1, -1.0)):
        message = message_ref[side, : 4 * members, :]
        for (i, f), value in edge_forecast(message, members, sign).items():
            row = i if sign > 0 else cells_x - 1 - i
            for c in range(0, cells_y, piece):
                dest, lane = spot(chunk, cells_y, row, f, c)
                at = (side, dest - side * (shards - touched), slice(None), slice(lane, lane + piece))
                block_ref[at] = block_ref[at] + value[:, c : c + piece]
        written.append(pltpu.make_async_copy(block_ref.at[side], out_ref.at[spans[side]], out_sems.at[side]))
        written[-1].start()
    for copy in written:
        copy.wait()


def column_of(row, lanes=128):
    return jnp.transpose(jnp.broadcast_to(row, (lanes,) + row.shape[1:]))


def gap2(a, b, around, inverse):
    gap = jnp.abs(a - b)
    gap = jnp.minimum(gap, around - gap) * inverse
    return gap * gap


def taper_of(squared):
    ramp = jnp.maximum(0.0, 1.0 - squared * lax.rsqrt(squared))
    return ramp * ramp


def geometry(owner_ref, offset_ref, cutoff_ref, b, slabs, cells_x, cells_y):
    offset = offset_ref[b : b + 1, :]
    row = lax.div(offset, cells_y) + owner_ref[b % slabs] * cells_x
    column = lax.rem(offset, cells_y)
    return row.astype(F32), column.astype(F32), 1.0 / cutoff_ref[b : b + 1, :].astype(F32)


def taper_kernel(slabs, cells_x, cells_y, batches, tile, groups, first_ref, owner_ref, offset_ref,
                 cutoff_ref, out_ref):
    starts = [first_ref[0] + at for at in groups]
    columns = {}
    for g, at in enumerate(groups):
        columns.setdefault(at % cells_y, []).append(g)
    for b in range(batches):
        row, column, inverse = (
            column_of(x) for x in geometry(owner_ref, offset_ref, cutoff_ref, b, slabs, cells_x, cells_y))
        rows = [gap2(lax.div(start, 3 * cells_y).astype(F32), row, float(cells_x * slabs), inverse)
                for start in starts]
        for members in columns.values():
            for lane in range(0, tile, 128):
                cell = (lax.rem(starts[members[0]], cells_y) + lane
                        + lax.broadcasted_iota(jnp.int32, (1, 128), 1)).astype(F32)
                gap_y = jnp.maximum(gap2(cell, column, float(cells_y), inverse), TINY)
                for g in members:
                    out_ref[g, b, :, lane : lane + 128] = taper_of(gap_y + rows[g])


def solve_members(gram, right, lowest, work_ref):
    size = gram.shape[0]
    top = jnp.max(jnp.sum(jnp.abs(gram), axis=1, keepdims=True), axis=0, keepdims=True)
    top = jnp.maximum(top, 4.0 * lowest)
    eye = jnp.where(
        lax.broadcasted_iota(jnp.int32, (size, size), 0)
        == lax.broadcasted_iota(jnp.int32, (size, size), 1), 1.0, 0.0)
    alpha = 2.0 / (top + lowest)

    def double(r, x, t):
        t = 2.0 * t * t - 1.0
        extra = 1.0 / t
        both = mm_f32(r, jnp.concatenate([r, x], axis=1))
        gain = 1.0 + extra
        return gain * both[:, :size] - extra * eye, gain * (x + both[:, size:]), t

    r, x, t = eye - alpha * gram, alpha * right, (top + lowest) / (top - lowest)
    for _ in range(ROUNDS):
        r, x, t = double(r, x, t)
    work_ref[:, :size] = r
    work_ref[:, size:] = x

    def more(t):
        r, x, t = double(work_ref[:, :size], work_ref[:, size:], jnp.full((1, 1), t, F32))
        work_ref[:, :size] = r
        work_ref[:, size:] = x
        return t[0, 0]

    lax.while_loop(lambda t: t < CONVERGED, more, t[0, 0])
    return work_ref[:, size:]


def stack3(state):
    high, low = split2(state - jnp.mean(state, axis=0, keepdims=True))
    return jnp.concatenate([high, low, high], axis=0)


def weigh(pair, high, low):
    members = pair.shape[0] // 2
    main, rest = mm(pair, high), mm(pair, low)
    return main[:members] + (main[members:] + rest[:members])


def chain_kernel(slabs, cells_x, cells_y, batches, parts, *refs):
    place_ref, owner_ref, offset_ref, cutoff_ref, values_ref, variance_ref, perturb_ref = refs[:7]
    part_refs = refs[7 : 7 + parts]
    y_ref, w_ref, obs_ref, work_ref = refs[7 + parts :]
    members = obs_ref.shape[0]
    nobs = offset_ref.shape[1]
    each = part_refs[0].shape[0]
    scale = 1.0 / (members - 1)
    each = each * cells_y // obs_ref.shape[1]
    for k in range(parts):
        at = pl.ds(pl.multiple_of(place_ref[k] * each, each), each)
        for c in range(obs_ref.shape[1] // cells_y):
            obs_ref[at, c * cells_y : (c + 1) * cells_y] = part_refs[k][c * each : (c + 1) * each, :]
    eye = (lax.broadcasted_iota(jnp.int32, (members, members), 0)
           == lax.broadcasted_iota(jnp.int32, (members, members), 1))
    places = [geometry(owner_ref, offset_ref, cutoff_ref, b, slabs, cells_x, cells_y)
              for b in range(batches)]
    for b in range(batches):
        observed = obs_ref[:, b * nobs : (b + 1) * nobs]
        spread = observed - jnp.mean(observed, axis=0, keepdims=True)
        variance = variance_ref[b : b + 1, :]
        inverse = 1.0 / variance
        target = values_ref[b : b + 1, :] + jnp.sqrt(variance) * perturb_ref[b] - observed
        both = mm_f32(spread * inverse, jnp.concatenate([spread, target], axis=0), ((1,), (1,)))
        gram = both[:, :members] + jnp.where(eye, float(members - 1), 0.0)
        high, low = split2(jnp.transpose(spread) * scale)
        spread_t = jnp.concatenate([high, high, low], axis=1)
        y_ref[b] = spread_t
        if b + 1 < batches:
            later = obs_ref[:, (b + 1) * nobs :]
            row, column, inverse_cutoff = (column_of(x) for x in places[b])
            tapers = []
            for c in range(b + 1, batches):
                for lane in range(0, nobs, 128):
                    row_j, column_j = (x[:, lane : lane + 128] for x in places[c][:2])
                    squared = (gap2(row_j, row, float(cells_x * slabs), inverse_cutoff)
                               + gap2(column_j, column, float(cells_y), inverse_cutoff))
                    tapers.append(taper_of(jnp.maximum(squared, TINY)))
            gain_high, gain_low = split2(
                mm(spread_t, stack3(later)) * jnp.concatenate(tapers, axis=1))
        solved = solve_members(gram, both[:, members:], float(members - 1), work_ref)
        weights = (target - mm_f32(solved, spread, ((0,), (0,)))) * inverse
        high, low = split2(weights)
        pair = jnp.concatenate([high, low], axis=0)
        w_ref[b] = pair
        if b + 1 < batches:
            obs_ref[:, (b + 1) * nobs :] = later + weigh(pair, gain_high, gain_low)


def update_kernel(batches, tile, groups, s_ref, y_ref, w_ref, taper_ref, out_ref):
    for b in range(batches):
        for g, tiles in enumerate(groups):
            for at in tiles:
                state = (out_ref if b else s_ref)[:, at : at + tile]
                covariance = mm(y_ref[b], stack3(state))
                high, low = split2(covariance * taper_ref[g, b])
                out_ref[:, at : at + tile] = state + weigh(w_ref[b], high, low)


def on_device(prior, obs_values, obs_variance, obs_perturb, obs_offset, owner_order, taper_cutoff):
    slabs = lax.axis_size("slab")
    shards = lax.axis_size("member")
    each, cells_x, _, cells_y = prior.shape
    batches, nobs = obs_values.shape
    members = each * shards
    chunk = 3 * cells_x * cells_y // shards
    slab = lax.axis_index("slab")
    member = lax.axis_index("member")
    x = prior.transpose(0, 2, 1, 3).reshape(each * 3 * cells_x, cells_y)
    owner = owner_order.astype(jnp.int32)
    perturb = obs_perturb.transpose(0, 2, 1)

    def shift(count, by):
        return [(i, (i + by) % count) for i in range(count)]

    lines = batches * nobs // cells_y * each
    message = jax.ShapeDtypeStruct((4 * each + lines, cells_y), F32)
    lane_tiles = (cells_y // 128, each * 3 * cells_x, 128)
    partial, to_next, to_prev, mid, rim = pl.pallas_call(
        functools.partial(prior_kernel, each, cells_x, slabs, batches),
        out_shape=(
            jax.ShapeDtypeStruct((lines, cells_y), F32), message, message,
            jax.ShapeDtypeStruct(lane_tiles, F32), jax.ShapeDtypeStruct((2 * each, cells_y), F32),
        ),
        in_specs=[SMEM_SPEC, SMEM_SPEC, VMEM_SPEC, VMEM_SPEC],
        out_specs=(VMEM_SPEC,) * 5,
        scratch_shapes=[
            pltpu.VMEM((each * cells_x + 6 * each, cells_y), F32),
            pltpu.VMEM(lane_tiles, F32),
        ],
        name="prior",
    )(slab.reshape(1), owner, x, obs_offset)
    low = lax.ppermute(to_next, "slab", shift(slabs, 1))
    high = lax.ppermute(to_prev, "slab", shift(slabs, -1))
    others = [lax.ppermute(partial, "slab", shift(slabs, by)) for by in range(2, slabs - 1)]

    outgoing = jax.ShapeDtypeStruct((shards, each, chunk), F32)
    inner = pl.pallas_call(
        functools.partial(forecast_kernel, each, cells_x),
        out_shape=outgoing,
        in_specs=[VMEM_SPEC] * 2,
        out_specs=VMEM_SPEC,
        scratch_shapes=[pltpu.VMEM((cells_y // 128, each * 2 * cells_x, 128), F32)],
        name="forecast",
    )(mid, rim)
    fixed = 3 + len(others)
    outgoing, observed = pl.pallas_call(
        functools.partial(correct_kernel, each, cells_x, len(others)),
        out_shape=(outgoing, jax.ShapeDtypeStruct((lines, cells_y), F32)),
        in_specs=[ANY_SPEC] * (fixed + 1),
        out_specs=(ANY_SPEC, VMEM_SPEC),
        input_output_aliases={fixed: 0},
        scratch_shapes=[
            pltpu.VMEM((2, 4 * each + lines, cells_y), F32),
            pltpu.VMEM((1 + len(others), lines, cells_y), F32),
            pltpu.VMEM((2, 4 * 3 * cells_y // chunk, each, chunk), F32),
            pltpu.SemaphoreType.DMA((fixed + 2,)),
            pltpu.SemaphoreType.DMA((2,)),
        ],
        name="correct",
    )(low, high, partial, *others, inner)

    pieces = [observed]
    for by in range(2, shards, 2):
        pieces.append(lax.ppermute(observed, "member", shift(shards, by)))
    swap = [(i, i ^ 1) for i in range(shards)]
    pieces += [lax.ppermute(p, "member", swap) for p in pieces]
    evens = jnp.arange(0, shards, 2, dtype=jnp.int32)
    place = lax.rem(jnp.concatenate([member - evens, (member ^ 1) - evens]) + shards, shards)

    state = lax.all_to_all(outgoing, "member", 0, 0).reshape(members, chunk)

    steps = max(1, chunk // (3 * cells_y))
    width = chunk // steps
    tile = math.gcd(width, 256)
    if width == 3 * cells_y:
        groups = [[f * cells_y + c for f in range(3)] for c in range(0, cells_y, tile)]
    else:
        groups = [[at] for at in range(0, width, tile)]
    firsts = [i * width + g[0] for i in range(steps) for g in groups]
    first = (slab * shards + member) * chunk
    taper = pl.pallas_call(
        functools.partial(
            taper_kernel, slabs, cells_x, cells_y, batches, tile, firsts),
        out_shape=jax.ShapeDtypeStruct((len(firsts), batches, nobs, tile), F32),
        in_specs=[SMEM_SPEC, SMEM_SPEC, VMEM_SPEC, VMEM_SPEC],
        out_specs=VMEM_SPEC,
        name="taper",
    )(first.reshape(1), owner, obs_offset, taper_cutoff)

    chain = pl.pallas_call(
        functools.partial(chain_kernel, slabs, cells_x, cells_y, batches, shards),
        out_shape=(
            jax.ShapeDtypeStruct((batches, nobs, 3 * members), BF16),
            jax.ShapeDtypeStruct((batches, 2 * members, nobs), BF16),
        ),
        in_specs=[SMEM_SPEC, SMEM_SPEC] + [VMEM_SPEC] * (5 + shards),
        out_specs=(VMEM_SPEC,) * 2,
        scratch_shapes=[
            pltpu.VMEM((members, batches * nobs), F32),
            pltpu.VMEM((members, 2 * members), F32),
        ],
        name="chain",
    )
    y_all, w_all = chain(
        place, owner, obs_offset, taper_cutoff, obs_values, obs_variance, perturb, *pieces)

    block = pl.BlockSpec((members, width), lambda i: (0, i))
    return pl.pallas_call(
        functools.partial(update_kernel, batches, tile, groups),
        grid=(steps,),
        out_shape=jax.ShapeDtypeStruct((members, chunk), F32),
        in_specs=[
            block, VMEM_SPEC, VMEM_SPEC,
            pl.BlockSpec((len(groups), batches, nobs, tile), lambda i: (i, 0, 0, 0)),
        ],
        out_specs=block,
        name="update",
    )(state, y_all, w_all, taper)


def solution(mesh):
    in_specs = (P("member", "slab", None, None), P(), P(), P(), P(), P(), P())
    out_specs = P(None, ("slab", "member"))

    return jax.shard_map(on_device, mesh=mesh, in_specs=in_specs, out_specs=out_specs, check_vma=False)
```

time: 76.6 us -> 69.3 us (0.905); the launches traced: 75.4 us -> 69 us
  waiting for transfers between devices: 8.99 us -> 19.4 us
  starting transfers between devices: 25.1 us -> 16.3 us
  Pallas kernels: 37.7 us -> 30.5 us
    ppermute x12 -> x10, waiting for transfers between devices: 8.99 us -> 19.4 us  [the longest x3 18.8 us: on_device(): pieces.append(lax.ppermute(observed, 'member', shift(shards, by)))]
    ppermute x12 -> x10, starting transfers between devices: 20.1 us -> 11.4 us  [the longest x3 4.95 us: on_device(): pieces.append(lax.ppermute(observed, 'member', shift(shards, by)))]
    pallas_call x2, Pallas kernels: 12.2 us -> 9.5 us  [the longest x1 6.62 us: on_device(): pl.pallas_call(functools.partial(update_kernel, batches, tile, groups), g...]
    pallas_call x1, Pallas kernels: 4.69 us -> 2.75 us  [on_device(): pl.pallas_call(functools.partial(forecast_kernel, each, cells_x), out_sha...]
    pallas_call x1, Pallas kernels: 11.9 us -> 10.5 us  [on_device(): chain(place, owner, obs_offset, taper_cutoff, obs_values, obs_variance, p...]
    pallas_call x1, Pallas kernels: 5.7 us -> 4.43 us  [on_device(): pl.pallas_call(functools.partial(taper_kernel, slabs, cells_x, cells_y, b...]
    add x1 -> x0, other arithmetic: 0.77 us -> none  [on_device(): observed = observed + permute(partial, 'slab', slabs, by)]
  transfers between devices with their start and end apart: 13 -> 11, of which waited for: 5 -> 3; matrix products, arithmetic and copies ran while one was open for 2% -> 1% of each run, Pallas kernels for 28% -> 26%
where the time goes in v3:
time: 69.3 us; the launch traced here: 69 us
  Pallas kernels  30.5 us (44%)
  waiting for transfers between devices  19.4 us (28%)
  starting transfers between devices  16.3 us (24%)
  local copies, waits for them, and re-layouts  2.13 us (3%)
    ppermute x3, waiting for transfers between devices, on_device(): pieces.append(lax.ppermute(observed, 'member', shift(shards, by)))  18.8 us
    pallas_call x1, Pallas kernels, on_device(): chain(place, owner, obs_offset, taper_cutoff, obs_values, obs_variance, p...  10.5 us
    pallas_call x1, Pallas kernels, on_device(): pl.pallas_call(functools.partial(update_kernel, batches, tile, groups), g...  6.62 us
    ppermute x3, starting transfers between devices, on_device(): pieces.append(lax.ppermute(observed, 'member', shift(shards, by)))  4.95 us
    all_to_all x1, starting transfers between devices, on_device(): state = lax.all_to_all(outgoing, 'member', 0, 0).reshape(members, chunk)  4.89 us
    pallas_call x1, Pallas kernels, on_device(): pl.pallas_call(functools.partial(taper_kernel, slabs, cells_x, cells_y, b...  4.43 us
    pallas_call x1, Pallas kernels, on_device(): pl.pallas_call(functools.partial(prior_kernel, each, cells_x, slabs, batc...  3.27 us
    ppermute x1, starting transfers between devices, on_device(): low = lax.ppermute(to_next, 'slab', shift(slabs, 1))  2.97 us
  transfers between devices with their start and end apart: 11, of which 3 were waited for; matrix products, arithmetic and copies ran while one was open for 1% of the time, Pallas kernels for 26%

profile of v3, /device:TPU:0, one launch (start us, length us, event | category | flops | bytes accessed | tf_op | source)
XLA Modules:
  0.0 69.0 jit_solution(12904338703778434674)
XLA Ops:
  0.0 3.3 %prior.1 = (f32[16,512]{1,0:T(8,128)}, f32[48,512]{1,0:T(8,128)}, f32[48,512]{1,0:T(8,128)}, f32[4,384,128]{2,1,0:T(8,128)}, f32[16,512]{1,0:T(8,128)}) custom-call(s32[1]{0:T(128)} %bitcast.me_ref, s32[4]{0:T(128)} %owner_ref.3, f32[384,512]{1,0:T(8,128)} %bitcast.8, s32[4,256]{1,0:T(4,128)} %offset_ref.3), custom_call_target="tpu_custom_call" | custom-call | tf_op jit(solution)/shard_map/prior/pallas_call | solution.py:413
  3.3 3.0 %collective-permute-start = (f32[48,512]{1,0:T(8,128)}, f32[48,512]{1,0:T(8,128)S(1)}, u32[]{:S(2)}, u32[]{:S(2)}) collective-permute-start(f32[48,512]{1,0:T(8,128)} %get-tuple-element.14), channel_id=1, source_target_pairs={{0,8},{8,16},{16,24},{24,0},{1,9},{9,17},{17,25},{25,1},{2,10},{10... | collective-permute-start | bytes 294920 | tf_op jit(solution)/shard_map/ppermute | solution.py:427
  6.2 1.0 %collective-permute-start.1 = (f32[48,512]{1,0:T(8,128)}, f32[48,512]{1,0:T(8,128)S(1)}, u32[]{:S(2)}, u32[]{:S(2)}) collective-permute-start(f32[48,512]{1,0:T(8,128)} %get-tuple-element.15), channel_id=1, source_target_pairs={{0,24},{8,0},{16,8},{24,16},{1,25},{9,1},{17,9},{25,17},{2,26},{10... | collective-permute-start | bytes 294920 | tf_op jit(solution)/shard_map/ppermute | solution.py:428
  7.2 2.0 %collective-permute-start.2 = (f32[16,512]{1,0:T(8,128)}, f32[16,512]{1,0:T(8,128)S(1)}, u32[]{:S(2)}, u32[]{:S(2)}) collective-permute-start(f32[16,512]{1,0:T(8,128)} %get-tuple-element.16.refs_2_), channel_id=1, source_target_pairs={{0,16},{8,24},{16,0},{24,8},{1,17},{9,25},{17,1},{25,9},{2,18},{10... | collective-permute-start | bytes 98312 | tf_op jit(solution)/shard_map/ppermute | solution.py:429
  9.2 2.7 %forecast.1.refs_4_ = f32[8,8,3072]{2,1,0:T(8,128)} custom-call(f32[4,384,128]{2,1,0:T(8,128)} %get-tuple-element.17.mid_ref, f32[16,512]{1,0:T(8,128)} %get-tuple-element.18.rim_ref), custom_call_target="tpu_custom_call" | custom-call | tf_op jit(solution)/shard_map/forecast/pallas_call | solution.py:432
  11.9 0.0 collective-permute-done.2.refs_3_
  11.9 0.0 copy-start.10
  11.9 0.0 collective-permute-done.refs_0_
  11.9 0.0 copy-start.1
  12.0 0.6 collective-permute-done.1.refs_1_
  12.6 0.0 copy-done.10
  12.6 0.0 copy-done.1
  12.6 0.0 copy-start.2
  12.6 0.6 copy-done.2
  13.2 2.9 %correct.1 = (f32[8,8,3072]{2,1,0:T(8,128)}, f32[16,512]{1,0:T(8,128)}) custom-call(f32[48,512]{1,0:T(8,128)} %copy-done.1, f32[48,512]{1,0:T(8,128)} %copy-done.2, f32[16,512]{1,0:T(8,128)} %get-tuple-element.16.refs_2_, f32[16,512]{1,0:T(8,128)} %copy-done.10, f32[8,8,3072]{2,1,0:T(8,128)} %forecast.1.refs_4_), custom_call_target="tpu_custom_call", output_to_operand_aliasing={{0}: (4, {})} | custom-call | tf_op jit(solution)/shard_map/correct/pallas_call | solution.py:441
  16.1 4.9 %all-to-all-start = ((f32[8,8,3072]{2,1,0:T(8,128)}), f32[8,8,3072]{2,1,0:T(8,128)S(1)}, u32[]{:S(2)}, u32[]{:S(2)}) async-start(f32[8,8,3072]{2,1,0:T(8,128)} %get-tuple-element.19), calls=%async_computation | async-start | bytes 1572864 | tf_op jit(solution)/shard_map/all_to_all | solution.py:465
  21.0 3.8 %collective-permute-start.5 = (f32[16,512]{1,0:T(8,128)}, f32[16,512]{1,0:T(8,128)S(1)}, u32[]{:S(2)}, u32[]{:S(2)}) collective-permute-start(f32[16,512]{1,0:T(8,128)} %get-tuple-element.20.refs_7_), channel_id=1, source_target_pairs={{0,6},{1,7},{2,0},{3,1},{4,2},{5,3},{6,4},{7,5},{8,14},{9,15},{10,... | collective-permute-start | bytes 98312 | tf_op jit(solution)/shard_map/ppermute | solution.py:459
  24.8 0.0 collective-permute-start.4
  24.8 1.1 %collective-permute-start.3 = (f32[16,512]{1,0:T(8,128)}, f32[16,512]{1,0:T(8,128)S(1)}, u32[]{:S(2)}, u32[]{:S(2)}) collective-permute-start(f32[16,512]{1,0:T(8,128)} %get-tuple-element.20.refs_7_), channel_id=1, source_target_pairs={{0,2},{1,3},{2,4},{3,5},{4,6},{5,7},{6,0},{7,1},{8,10},{9,11},{10,... | collective-permute-start | bytes 98312 | tf_op jit(solution)/shard_map/ppermute | solution.py:459
  26.0 0.0 collective-permute-start.6
  26.0 9.8 %collective-permute-done.5.refs_10_ = f32[16,512]{1,0:T(8,128)S(1)} collective-permute-done((f32[16,512]{1,0:T(8,128)}, f32[16,512]{1,0:T(8,128)S(1)}, u32[]{:S(2)}, u32[]{:S(2)}) %collective-permute-start.5) | collective-permute-done | bytes 32800 | tf_op jit(solution)/shard_map/ppermute | solution.py:459
  35.8 0.0 copy-start.3
  35.8 0.0 collective-permute-start.9
  35.8 9.0 %collective-permute-done.4.refs_9_ = f32[16,512]{1,0:T(8,128)S(1)} collective-permute-done((f32[16,512]{1,0:T(8,128)}, f32[16,512]{1,0:T(8,128)S(1)}, u32[]{:S(2)}, u32[]{:S(2)}) %collective-permute-start.4) | collective-permute-done | bytes 32800 | tf_op jit(solution)/shard_map/ppermute | solution.py:459
  44.8 0.0 copy-start.4
  44.8 0.0 collective-permute-start.8
  44.8 0.0 collective-permute-done.3.refs_8_
  44.8 0.0 copy-start.5
  44.8 0.5 collective-permute-start.7
  45.3 0.6 compare_select_fusion.refs_0_
  45.9 4.4 %taper.1.taper_ref = f32[4,4,256,256]{3,2,1,0:T(8,128)} custom-call(s32[1]{0:T(128)} %bitcast.5.first_ref, s32[4]{0:T(128)} %owner_ref.3, s32[4,256]{1,0:T(4,128)} %offset_ref.3, s32[4,256]{1,0:T(4,128)} %cutoff_ref.1), custom_call_target="tpu_custom_call" | custom-call | tf_op jit(solution)/shard_map/taper/pallas_call | solution.py:476
  50.3 0.0 collective-permute-done.6.refs_11_
  50.3 0.0 copy-start.6
  50.3 0.0 collective-permute-done.9.refs_14_
  50.3 0.0 copy-start.7
  50.3 0.0 collective-permute-done.8.refs_13_
  50.3 0.0 copy-start.8
  50.3 0.0 collective-permute-done.7.refs_12_
  50.4 0.0 copy-start.9
  50.4 0.0 copy-done.3
  50.4 0.0 copy-done.4
  50.4 0.0 copy-done.5
  50.4 0.5 copy-done.6
  50.9 0.0 copy-done.7
  50.9 0.0 copy-done.8
  51.0 0.0 copy-done.9
  51.0 10.5 %chain.1 = (bf16[4,256,192]{2,1,0:T(8,128)(2,1)}, bf16[4,128,256]{2,1,0:T(8,128)(2,1)}) custom-call(s32[8]{0:T(128)} %compare_select_fusion.refs_0_, s32[4]{0:T(128)} %owner_ref.3, s32[4,256]{1,0:T(4,128)} %offset_ref.3, s32[4,256]{1,0:T(4,128)} %cutoff_ref.1, f32[4,256]{1,0:T(4,128)} %refs_4_.1, f32[4,256]{1,0:T(4,128)} %refs_5_.1, f32[4,64,256]{2,1,0:T(8,128)} %bitcast.9, ...), custom_call_target="tpu_custom_call" | custom-call | tf_op jit(solution)/shard_map/chain/pallas_call | solution.py:499
  61.5 0.0 all-to-all-done
  61.5 0.0 copy-start
  61.5 0.9 %copy-done = f32[8,8,3072]{2,1,0:T(8,128)} copy-done((f32[8,8,3072]{2,1,0:T(8,128)}, f32[8,8,3072]{2,1,0:T(8,128)S(1)}, u32[]{:S(2)}) %copy-start) | copy-done | bytes 786456
  62.4 6.6 %update.1 = f32[64,3072]{1,0:T(8,128)} custom-call(f32[64,3072]{1,0:T(8,128)} %bitcast.7, bf16[4,256,192]{2,1,0:T(8,128)(2,1)} %get-tuple-element.21.y_ref, bf16[4,128,256]{2,1,0:T(8,128)(2,1)} %get-tuple-element.22.w_ref, f32[4,4,256,256]{3,2,1,0:T(8,128)} %taper.1.taper_ref), custom_call_target="tpu_custom_call" | custom-call | tf_op jit(solution)/shard_map/update/pallas_call | solution.py:503
  (1 shorter events, 0.0 us)
Async XLA Ops:
  3.3 8.7 %collective-permute-start = (f32[48,512]{1,0:T(8,128)}, f32[48,512]{1,0:T(8,128)S(1)}, u32[]{:S(2)}, u32[]{:S(2)}) collective-permute-start(f32[48,512]{1,0:T(8,128)} %get-tuple-element.14), channel_id=1, source_target_pairs={{0,8},{8,16},{16,24},{24,0},{1,9},{9,17},{17,25},{25,1},{2,10},{10... | collective-permute-start | bytes 294920 | tf_op jit(solution)/shard_map/ppermute | solution.py:427
  6.2 6.3 %collective-permute-start.1 = (f32[48,512]{1,0:T(8,128)}, f32[48,512]{1,0:T(8,128)S(1)}, u32[]{:S(2)}, u32[]{:S(2)}) collective-permute-start(f32[48,512]{1,0:T(8,128)} %get-tuple-element.15), channel_id=1, source_target_pairs={{0,24},{8,0},{16,8},{24,16},{1,25},{9,1},{17,9},{25,17},{2,26},{10... | collective-permute-start | bytes 294920 | tf_op jit(solution)/shard_map/ppermute | solution.py:428
  7.2 4.7 %collective-permute-start.2 = (f32[16,512]{1,0:T(8,128)}, f32[16,512]{1,0:T(8,128)S(1)}, u32[]{:S(2)}, u32[]{:S(2)}) collective-permute-start(f32[16,512]{1,0:T(8,128)} %get-tuple-element.16.refs_2_), channel_id=1, source_target_pairs={{0,16},{8,24},{16,0},{24,8},{1,17},{9,25},{17,1},{25,9},{2,18},{10... | collective-permute-start | bytes 98312 | tf_op jit(solution)/shard_map/ppermute | solution.py:429
  11.9 0.6 copy-start.10
  11.9 0.6 copy-start.1
  12.6 0.6 copy-start.2
  16.1 45.4 %all-to-all-start = ((f32[8,8,3072]{2,1,0:T(8,128)}), f32[8,8,3072]{2,1,0:T(8,128)S(1)}, u32[]{:S(2)}, u32[]{:S(2)}) async-start(f32[8,8,3072]{2,1,0:T(8,128)} %get-tuple-element.19), calls=%async_computation | async-start | bytes 1572864 | tf_op jit(solution)/shard_map/all_to_all | solution.py:465
  21.0 14.8 %collective-permute-start.5 = (f32[16,512]{1,0:T(8,128)}, f32[16,512]{1,0:T(8,128)S(1)}, u32[]{:S(2)}, u32[]{:S(2)}) collective-permute-start(f32[16,512]{1,0:T(8,128)} %get-tuple-element.20.refs_7_), channel_id=1, source_target_pairs={{0,6},{1,7},{2,0},{3,1},{4,2},{5,3},{6,4},{7,5},{8,14},{9,15},{10,... | collective-permute-start | bytes 98312 | tf_op jit(solution)/shard_map/ppermute | solution.py:459
  24.8 19.9 %collective-permute-start.4 = (f32[16,512]{1,0:T(8,128)}, f32[16,512]{1,0:T(8,128)S(1)}, u32[]{:S(2)}, u32[]{:S(2)}) collective-permute-start(f32[16,512]{1,0:T(8,128)} %get-tuple-element.20.refs_7_), channel_id=1, source_target_pairs={{0,4},{1,5},{2,6},{3,7},{4,0},{5,1},{6,2},{7,3},{8,12},{9,13},{10,... | collective-permute-start | bytes 98312 | tf_op jit(solution)/shard_map/ppermute | solution.py:459
  24.8 19.9 %collective-permute-start.3 = (f32[16,512]{1,0:T(8,128)}, f32[16,512]{1,0:T(8,128)S(1)}, u32[]{:S(2)}, u32[]{:S(2)}) collective-permute-start(f32[16,512]{1,0:T(8,128)} %get-tuple-element.20.refs_7_), channel_id=1, source_target_pairs={{0,2},{1,3},{2,4},{3,5},{4,6},{5,7},{6,0},{7,1},{8,10},{9,11},{10,... | collective-permute-start | bytes 98312 | tf_op jit(solution)/shard_map/ppermute | solution.py:459
  26.0 24.4 %collective-permute-start.6 = (f32[16,512]{1,0:T(8,128)}, f32[16,512]{1,0:T(8,128)S(1)}, u32[]{:S(2)}, u32[]{:S(2)}) collective-permute-start(f32[16,512]{1,0:T(8,128)} %get-tuple-element.20.refs_7_), channel_id=1, source_target_pairs={{0,1},{1,0},{2,3},{3,2},{4,5},{5,4},{6,7},{7,6},{8,9},{9,8},{10,11... | collective-permute-start | bytes 98312 | tf_op jit(solution)/shard_map/ppermute | solution.py:461
  35.8 14.6 %copy-start.3 = (f32[16,512]{1,0:T(8,128)}, f32[16,512]{1,0:T(8,128)S(1)}, u32[]{:S(2)}) copy-start(f32[16,512]{1,0:T(8,128)S(1)} %collective-permute-done.5.refs_10_) | copy-start | bytes 98308
  35.8 14.5 %collective-permute-start.9 = (f32[16,512]{1,0:T(8,128)S(1)}, f32[16,512]{1,0:T(8,128)S(1)}, u32[]{:S(2)}, u32[]{:S(2)}) collective-permute-start(f32[16,512]{1,0:T(8,128)S(1)} %collective-permute-done.5.refs_10_), channel_id=1, source_target_pairs={{0,1},{1,0},{2,3},{3,2},{4,5},{5,4},{6,7},{7,6},{8,9},{9,8},{10,11... | collective-permute-start | bytes 98312 | tf_op jit(solution)/shard_map/ppermute | solution.py:461
  44.8 5.6 %copy-start.4 = (f32[16,512]{1,0:T(8,128)}, f32[16,512]{1,0:T(8,128)S(1)}, u32[]{:S(2)}) copy-start(f32[16,512]{1,0:T(8,128)S(1)} %collective-permute-done.4.refs_9_) | copy-start | bytes 98308
  44.8 5.6 %collective-permute-start.8 = (f32[16,512]{1,0:T(8,128)S(1)}, f32[16,512]{1,0:T(8,128)S(1)}, u32[]{:S(2)}, u32[]{:S(2)}) collective-permute-start(f32[16,512]{1,0:T(8,128)S(1)} %collective-permute-done.4.refs_9_), channel_id=1, source_target_pairs={{0,1},{1,0},{2,3},{3,2},{4,5},{5,4},{6,7},{7,6},{8,9},{9,8},{10,11... | collective-permute-start | bytes 98312 | tf_op jit(solution)/shard_map/ppermute | solution.py:461
  44.8 5.6 %copy-start.5 = (f32[16,512]{1,0:T(8,128)}, f32[16,512]{1,0:T(8,128)S(1)}, u32[]{:S(2)}) copy-start(f32[16,512]{1,0:T(8,128)S(1)} %collective-permute-done.3.refs_8_) | copy-start | bytes 98308
  44.8 5.6 %collective-permute-start.7 = (f32[16,512]{1,0:T(8,128)S(1)}, f32[16,512]{1,0:T(8,128)S(1)}, u32[]{:S(2)}, u32[]{:S(2)}) collective-permute-start(f32[16,512]{1,0:T(8,128)S(1)} %collective-permute-done.3.refs_8_), channel_id=1, source_target_pairs={{0,1},{1,0},{2,3},{3,2},{4,5},{5,4},{6,7},{7,6},{8,9},{9,8},{10,11... | collective-permute-start | bytes 98312 | tf_op jit(solution)/shard_map/ppermute | solution.py:461
  50.3 0.6 copy-start.6
  50.3 0.6 copy-start.7
  50.3 0.6 copy-start.8
  50.4 0.6 copy-start.9
  61.5 0.9 %copy-start = (f32[8,8,3072]{2,1,0:T(8,128)}, f32[8,8,3072]{2,1,0:T(8,128)S(1)}, u32[]{:S(2)}) copy-start(f32[8,8,3072]{2,1,0:T(8,128)S(1)} %all-to-all-done) | copy-start | bytes 2359300

commit v4 on v3

--- a/solution.py
+++ b/solution.py
@@ -14,12 +14,24 @@
 HALF = COURANT * 0.5
 ROUNDS = 6
 TINY = 1e-30
+KERNEL_VMEM = 40 * 1024 * 1024
 CONVERGED = 1e6
 F32 = jnp.float32
 BF16 = jnp.bfloat16
 VMEM_SPEC = pl.BlockSpec(memory_space=pltpu.VMEM)
-ANY_SPEC = pl.BlockSpec(memory_space=pl.ANY)
 SMEM_SPEC = pl.BlockSpec(memory_space=pltpu.SMEM)
+
+
+def near(*arrays):
+    return [pltpu.with_memory_space_constraint(x, pltpu.VMEM) for x in arrays]
+
+
+def far(*arrays):
+    return [pltpu.with_memory_space_constraint(x, pltpu.HBM) for x in arrays]
+
+
+def kernel_params(limit=KERNEL_VMEM):
+    return pltpu.CompilerParams(vmem_limit_bytes=limit)
 
 
 def d_y(field, scale=1.0):
@@ -149,8 +161,6 @@
         at = b * nobs
         place = (pl.ds(at // cells_y * members, members), slice(at % cells_y, at % cells_y + nobs))
         obs_ref[place] = whole
-        for out_ref in (next_ref, prev_ref):
-            out_ref[pl.ds(4 * members + at // cells_y * members, members), place[1]] = whole
 
 
 def spot(chunk, cells_y, row, field, column):
@@ -211,40 +221,31 @@
     }
 
 
-def correct_kernel(members, cells_x, others, *refs):
-    low_ref, high_ref, partial_ref = refs[:3]
-    other_refs, in_ref = refs[3 : 3 + others], refs[3 + others]
-    out_ref, sum_ref, message_ref, obs_ref, block_ref, in_sems, out_sems = refs[4 + others :]
-    cells_y = sum_ref.shape[1]
-    shards, _, chunk = in_ref.shape
-    touched = block_ref.shape[1]
+def correct_kernel(members, cells_x, low_ref, high_ref, in_ref, out_ref):
+    cells_y = low_ref.shape[1]
+    chunk = out_ref.shape[2]
     piece = math.gcd(chunk, cells_y)
-    spans = [pl.ds(0, touched), pl.ds(shards - touched, touched)]
-    moves = [(low_ref, message_ref.at[0]), (high_ref, message_ref.at[1]), (partial_ref, obs_ref.at[0])]
-    moves += [(ref, obs_ref.at[1 + i]) for i, ref in enumerate(other_refs)]
-    moves += [(in_ref.at[spans[i]], block_ref.at[i]) for i in range(2)]
-    copies = [pltpu.make_async_copy(a, b, in_sems.at[i]) for i, (a, b) in enumerate(moves)]
-    for copy in copies:
-        copy.start()
-    for copy in copies:
-        copy.wait()
-    total = message_ref[0, 4 * members :, :] + message_ref[1, 4 * members :, :]
-    for i in range(1 + others):
-        total = total + obs_ref[i]
-    sum_ref[...] = total
-    written = []
-    for side, sign in ((0, 1.0), (1, -1.0)):
-        message = message_ref[side, : 4 * members, :]
-        for (i, f), value in edge_forecast(message, members, sign).items():
+    out_ref[...] = in_ref[...]
+    for ref, sign in ((low_ref, 1.0), (high_ref, -1.0)):
+        for (i, f), value in edge_forecast(ref[...], members, sign).items():
             row = i if sign > 0 else cells_x - 1 - i
             for c in range(0, cells_y, piece):
                 dest, lane = spot(chunk, cells_y, row, f, c)
-                at = (side, dest - side * (shards - touched), slice(None), slice(lane, lane + piece))
-                block_ref[at] = block_ref[at] + value[:, c : c + piece]
-        written.append(pltpu.make_async_copy(block_ref.at[side], out_ref.at[spans[side]], out_sems.at[side]))
-        written[-1].start()
-    for copy in written:
-        copy.wait()
+                at = (dest, slice(None), slice(lane, lane + piece))
+                out_ref[at] = in_ref[at] + value[:, c : c + piece]
+
+
+def stack_kernel(*refs):
+    rows = refs[0].shape[0]
+    for k, ref in enumerate(refs[:-1]):
+        refs[-1][k * rows : (k + 1) * rows, :] = ref[...]
+
+
+def sum_kernel(*refs):
+    total = refs[0][...]
+    for ref in refs[1:-1]:
+        total = total + ref[...]
+    refs[-1][...] = total
 
 
 def column_of(row, lanes=128):
@@ -333,18 +334,20 @@
 
 
 def chain_kernel(slabs, cells_x, cells_y, batches, parts, *refs):
-    place_ref, owner_ref, offset_ref, cutoff_ref, values_ref, variance_ref, perturb_ref = refs[:7]
-    part_refs = refs[7 : 7 + parts]
-    y_ref, w_ref, obs_ref, work_ref = refs[7 + parts :]
+    member_ref, owner_ref, offset_ref, cutoff_ref, values_ref, variance_ref, perturb_ref = refs[:7]
+    y_ref, w_ref, obs_ref, work_ref = refs[9:]
     members = obs_ref.shape[0]
     nobs = offset_ref.shape[1]
-    each = part_refs[0].shape[0]
+    each = members // parts
     scale = 1.0 / (members - 1)
-    each = each * cells_y // obs_ref.shape[1]
+    blocks = obs_ref.shape[1] // cells_y
     for k in range(parts):
-        at = pl.ds(pl.multiple_of(place_ref[k] * each, each), each)
-        for c in range(obs_ref.shape[1] // cells_y):
-            obs_ref[at, c * cells_y : (c + 1) * cells_y] = part_refs[k][c * each : (c + 1) * each, :]
+        half, by = divmod(k, parts // 2)
+        source = lax.rem((member_ref[0] ^ half) - 2 * by + parts, parts)
+        at = pl.ds(pl.multiple_of(source * each, each), each)
+        for c in range(blocks):
+            first = (by * blocks + c) * each
+            obs_ref[at, c * cells_y : (c + 1) * cells_y] = refs[7 + half][first : first + each, :]
     eye = (lax.broadcasted_iota(jnp.int32, (members, members), 0)
            == lax.broadcasted_iota(jnp.int32, (members, members), 1))
     places = [geometry(owner_ref, offset_ref, cutoff_ref, b, slabs, cells_x, cells_y)
@@ -382,10 +385,15 @@
 
 
 def update_kernel(batches, tile, groups, s_ref, y_ref, w_ref, taper_ref, out_ref):
+    step = pl.program_id(0)
+    width = out_ref.shape[1]
     for b in range(batches):
         for g, tiles in enumerate(groups):
             for at in tiles:
-                state = (out_ref if b else s_ref)[:, at : at + tile]
+                if b:
+                    state = out_ref[:, at : at + tile]
+                else:
+                    state = s_ref[:, pl.ds(pl.multiple_of(step * width + at, 128), tile)]
                 covariance = mm(y_ref[b], stack3(state))
                 high, low = split2(covariance * taper_ref[g, b])
                 out_ref[:, at : at + tile] = state + weigh(w_ref[b], high, low)
@@ -408,13 +416,13 @@
         return [(i, (i + by) % count) for i in range(count)]
 
     lines = batches * nobs // cells_y * each
-    message = jax.ShapeDtypeStruct((4 * each + lines, cells_y), F32)
+    message = pltpu.VMEM((4 * each, cells_y), F32)
     lane_tiles = (cells_y // 128, each * 3 * cells_x, 128)
     partial, to_next, to_prev, mid, rim = pl.pallas_call(
         functools.partial(prior_kernel, each, cells_x, slabs, batches),
         out_shape=(
-            jax.ShapeDtypeStruct((lines, cells_y), F32), message, message,
-            jax.ShapeDtypeStruct(lane_tiles, F32), jax.ShapeDtypeStruct((2 * each, cells_y), F32),
+            pltpu.VMEM((lines, cells_y), F32), message, message,
+            pltpu.VMEM(lane_tiles, F32), pltpu.VMEM((2 * each, cells_y), F32),
         ),
         in_specs=[SMEM_SPEC, SMEM_SPEC, VMEM_SPEC, VMEM_SPEC],
         out_specs=(VMEM_SPEC,) * 5,
@@ -422,47 +430,46 @@
             pltpu.VMEM((each * cells_x + 6 * each, cells_y), F32),
             pltpu.VMEM(lane_tiles, F32),
         ],
+        compiler_params=kernel_params(),
         name="prior",
-    )(slab.reshape(1), owner, x, obs_offset)
+    )(slab.reshape(1), *far(owner, x, obs_offset))
     low = lax.ppermute(to_next, "slab", shift(slabs, 1))
     high = lax.ppermute(to_prev, "slab", shift(slabs, -1))
-    others = [lax.ppermute(partial, "slab", shift(slabs, by)) for by in range(2, slabs - 1)]
-
-    outgoing = jax.ShapeDtypeStruct((shards, each, chunk), F32)
+    pieces = [partial] + [
+        lax.ppermute(partial, "member", shift(shards, by)) for by in range(2, shards, 2)]
+
+    outgoing = pltpu.VMEM((shards, each, chunk), F32)
     inner = pl.pallas_call(
         functools.partial(forecast_kernel, each, cells_x),
         out_shape=outgoing,
         in_specs=[VMEM_SPEC] * 2,
         out_specs=VMEM_SPEC,
         scratch_shapes=[pltpu.VMEM((cells_y // 128, each * 2 * cells_x, 128), F32)],
+        compiler_params=kernel_params(),
         name="forecast",
-    )(mid, rim)
-    fixed = 3 + len(others)
-    outgoing, observed = pl.pallas_call(
-        functools.partial(correct_kernel, each, cells_x, len(others)),
-        out_shape=(outgoing, jax.ShapeDtypeStruct((lines, cells_y), F32)),
-        in_specs=[ANY_SPEC] * (fixed + 1),
-        out_specs=(ANY_SPEC, VMEM_SPEC),
-        input_output_aliases={fixed: 0},
-        scratch_shapes=[
-            pltpu.VMEM((2, 4 * each + lines, cells_y), F32),
-            pltpu.VMEM((1 + len(others), lines, cells_y), F32),
-            pltpu.VMEM((2, 4 * 3 * cells_y // chunk, each, chunk), F32),
-            pltpu.SemaphoreType.DMA((fixed + 2,)),
-            pltpu.SemaphoreType.DMA((2,)),
-        ],
+    )(*near(mid, rim))
+    outgoing = pl.pallas_call(
+        functools.partial(correct_kernel, each, cells_x),
+        out_shape=outgoing,
+        in_specs=[VMEM_SPEC] * 3,
+        out_specs=VMEM_SPEC,
+        compiler_params=kernel_params(),
         name="correct",
-    )(low, high, partial, *others, inner)
-
-    pieces = [observed]
-    for by in range(2, shards, 2):
-        pieces.append(lax.ppermute(observed, "member", shift(shards, by)))
-    swap = [(i, i ^ 1) for i in range(shards)]
-    pieces += [lax.ppermute(p, "member", swap) for p in pieces]
-    evens = jnp.arange(0, shards, 2, dtype=jnp.int32)
-    place = lax.rem(jnp.concatenate([member - evens, (member ^ 1) - evens]) + shards, shards)
+    )(*near(low, high, inner))
 
     state = lax.all_to_all(outgoing, "member", 0, 0).reshape(members, chunk)
+
+    gathered = pltpu.VMEM((len(pieces) * lines, cells_y), F32)
+    stacked = pl.pallas_call(
+        stack_kernel, out_shape=gathered, in_specs=[VMEM_SPEC] * len(pieces), out_specs=VMEM_SPEC,
+        compiler_params=kernel_params(), name="stack",
+    )(*near(*pieces))
+    parts = [stacked] + [lax.ppermute(stacked, "slab", shift(slabs, by)) for by in range(1, slabs)]
+    observed = pl.pallas_call(
+        sum_kernel, out_shape=gathered, in_specs=[VMEM_SPEC] * slabs, out_specs=VMEM_SPEC,
+        compiler_params=kernel_params(), name="sum",
+    )(*near(*parts))
+    partner = lax.ppermute(observed, "member", [(i, i ^ 1) for i in range(shards)])
 
     steps = max(1, chunk // (3 * cells_y))
     width = chunk // steps
@@ -476,41 +483,41 @@
     taper = pl.pallas_call(
         functools.partial(
             taper_kernel, slabs, cells_x, cells_y, batches, tile, firsts),
-        out_shape=jax.ShapeDtypeStruct((len(firsts), batches, nobs, tile), F32),
+        out_shape=pltpu.HBM((len(firsts), batches, nobs, tile), F32),
         in_specs=[SMEM_SPEC, SMEM_SPEC, VMEM_SPEC, VMEM_SPEC],
         out_specs=VMEM_SPEC,
+        compiler_params=kernel_params(),
         name="taper",
     )(first.reshape(1), owner, obs_offset, taper_cutoff)
 
     chain = pl.pallas_call(
         functools.partial(chain_kernel, slabs, cells_x, cells_y, batches, shards),
         out_shape=(
-            jax.ShapeDtypeStruct((batches, nobs, 3 * members), BF16),
-            jax.ShapeDtypeStruct((batches, 2 * members, nobs), BF16),
+            pltpu.VMEM((batches, nobs, 3 * members), BF16),
+            pltpu.VMEM((batches, 2 * members, nobs), BF16),
         ),
-        in_specs=[SMEM_SPEC, SMEM_SPEC] + [VMEM_SPEC] * (5 + shards),
+        in_specs=[SMEM_SPEC, SMEM_SPEC] + [VMEM_SPEC] * 7,
         out_specs=(VMEM_SPEC,) * 2,
         scratch_shapes=[
             pltpu.VMEM((members, batches * nobs), F32),
             pltpu.VMEM((members, 2 * members), F32),
         ],
+        compiler_params=kernel_params(),
         name="chain",
     )
     y_all, w_all = chain(
-        place, owner, obs_offset, taper_cutoff, obs_values, obs_variance, perturb, *pieces)
+        member.reshape(1), owner, obs_offset, taper_cutoff, obs_values, obs_variance, perturb, *near(observed, partner))
 
     block = pl.BlockSpec((members, width), lambda i: (0, i))
     return pl.pallas_call(
         functools.partial(update_kernel, batches, tile, groups),
         grid=(steps,),
         out_shape=jax.ShapeDtypeStruct((members, chunk), F32),
-        in_specs=[
-            block, VMEM_SPEC, VMEM_SPEC,
-            pl.BlockSpec((len(groups), batches, nobs, tile), lambda i: (i, 0, 0, 0)),
-        ],
+        in_specs=[VMEM_SPEC] * 3 + [pl.BlockSpec((len(groups), batches, nobs, tile), lambda i: (i, 0, 0, 0))],
         out_specs=block,
+        compiler_params=kernel_params(),
         name="update",
-    )(state, y_all, w_all, taper)
+    )(*near(state, y_all, w_all), *far(taper))
 
 
 def solution(mesh):

time: 69.3 us -> 70.2 us (1.013)
  waiting for transfers between devices: 19.4 us -> 28 us
  Pallas kernels: 30.5 us -> 24.4 us
  local copies, waits for them, and re-layouts: 2.13 us -> 0.03 us
  starting transfers between devices: 16.3 us -> 17.4 us
    ppermute x8 -> x7, waiting for transfers between devices: 18.8 us -> 25.1 us  [the longest x3 18.8 us: on_device(): lax.ppermute(partial, 'member', shift(shards, by))]
    pallas_call x2 -> x4, Pallas kernels: 13.4 us -> 10.4 us  [the longest x1 9.24 us: on_device(): chain(member.reshape(1), owner, obs_offset, taper_cutoff, obs_values, obs...]
    unnamed x22 -> x12, local copies, waits for them, and re-layouts: 2.13 us -> 0.03 us
    pallas_call x1, Pallas kernels: 2.75 us -> 0.73 us  [on_device(): pl.pallas_call(functools.partial(forecast_kernel, each, cells_x), out_sha...]
    ppermute x1, waiting for transfers between devices: 0.01 us -> 1.49 us  [on_device(): low = lax.ppermute(to_next, 'slab', shift(slabs, 1))]
    ppermute x8 -> x7, starting transfers between devices: 7.42 us -> 8.49 us  [the longest x3 4.95 us: on_device(): lax.ppermute(partial, 'member', shift(shards, by))]
    ppermute x1, waiting for transfers between devices: 0.59 us -> 1.41 us  [on_device(): high = lax.ppermute(to_prev, 'slab', shift(slabs, -1))]
  transfers between devices with their start and end apart: 11 -> 10, of which waited for: 3 -> 6; matrix products, arithmetic and copies ran while one was open for 1% -> 0% of each run, Pallas kernels for 26% -> 20%
where the time goes in v4:
time: 70.2 us; the launch traced here: 70 us
  waiting for transfers between devices  28 us (40%)
  Pallas kernels  24.4 us (35%)
  starting transfers between devices  17.4 us (25%)
    ppermute x3, waiting for transfers between devices, on_device(): lax.ppermute(partial, 'member', shift(shards, by))  18.8 us
    pallas_call x1, Pallas kernels, on_device(): chain(member.reshape(1), owner, obs_offset, taper_cutoff, obs_values, obs...  9.24 us
    pallas_call x1, Pallas kernels, on_device(): pl.pallas_call(functools.partial(update_kernel, batches, tile, groups), g...  6.37 us
    ppermute x3, waiting for transfers between devices, on_device(): lax.ppermute(stacked, 'slab', shift(slabs, by))  6.25 us
    ppermute x3, starting transfers between devices, on_device(): lax.ppermute(partial, 'member', shift(shards, by))  4.95 us
    all_to_all x1, starting transfers between devices, on_device(): state = lax.all_to_all(outgoing, 'member', 0, 0).reshape(members, chunk)  4.88 us
    pallas_call x1, Pallas kernels, on_device(): pl.pallas_call(functools.partial(taper_kernel, slabs, cells_x, cells_y, b...  4.28 us
    ppermute x3, starting transfers between devices, on_device(): lax.ppermute(stacked, 'slab', shift(slabs, by))  3.47 us
  transfers between devices with their start and end apart: 10, of which 6 were waited for; matrix products, arithmetic and copies ran while one was open for 0% of the time, Pallas kernels for 20%

profile of v4, /device:TPU:0, one launch (start us, length us, event | category | flops | bytes accessed | tf_op | source)
XLA Modules:
  0.0 70.0 jit_solution(4876318802213373482)
XLA Ops:
  0.0 0.0 copy-start.3
  0.0 0.0 copy-start.1
  0.0 0.0 copy-start.2
  0.0 2.6 %prior.1 = (f32[16,512]{1,0:T(8,128)S(1)}, f32[32,512]{1,0:T(8,128)S(1)}, f32[32,512]{1,0:T(8,128)S(1)}, f32[4,384,128]{2,1,0:T(8,128)S(1)}, f32[16,512]{1,0:T(8,128)S(1)}) custom-call(s32[1]{0:T(128)} %bitcast.me_ref, s32[4]{0:T(128)} %owner_ref.3, f32[384,512]{1,0:T(8,128)} %bitcast.10, s32[4,256]{1,0:T(4,128)} %offset_ref.3), custom_call_target="tpu_custom_call" | custom-call | tf_op jit(solution)/shard_map/prior/pallas_call | solution.py:421
  2.6 3.0 %collective-permute-start = (f32[32,512]{1,0:T(8,128)S(1)}, f32[32,512]{1,0:T(8,128)S(1)}, u32[]{:S(2)}, u32[]{:S(2)}) collective-permute-start(f32[32,512]{1,0:T(8,128)S(1)} %get-tuple-element.12), channel_id=1, source_target_pairs={{0,8},{8,16},{16,24},{24,0},{1,9},{9,17},{17,25},{25,1},{2,10},{10... | collective-permute-start | bytes 196616 | tf_op jit(solution)/shard_map/ppermute | solution.py:436
  5.7 1.0 %collective-permute-start.1 = (f32[32,512]{1,0:T(8,128)S(1)}, f32[32,512]{1,0:T(8,128)S(1)}, u32[]{:S(2)}, u32[]{:S(2)}) collective-permute-start(f32[32,512]{1,0:T(8,128)S(1)} %get-tuple-element.13), channel_id=1, source_target_pairs={{0,24},{8,0},{16,8},{24,16},{1,25},{9,1},{17,9},{25,17},{2,26},{10... | collective-permute-start | bytes 196616 | tf_op jit(solution)/shard_map/ppermute | solution.py:437
  6.7 0.7 %forecast.1.in_ref = f32[8,8,3072]{2,1,0:T(8,128)S(1)} custom-call(f32[4,384,128]{2,1,0:T(8,128)S(1)} %get-tuple-element.14.mid_ref, f32[16,512]{1,0:T(8,128)S(1)} %get-tuple-element.15.rim_ref), custom_call_target="tpu_custom_call" | custom-call | tf_op jit(solution)/shard_map/forecast/pallas_call | solution.py:442
  7.4 0.0 copy-start
  7.4 0.0 copy-start.4
  7.4 0.0 copy-start.5
  7.5 1.5 %collective-permute-done.low_ref = f32[32,512]{1,0:T(8,128)S(1)} collective-permute-done((f32[32,512]{1,0:T(8,128)S(1)}, f32[32,512]{1,0:T(8,128)S(1)}, u32[]{:S(2)}, u32[]{:S(2)}) %collective-permute-start) | collective-permute-done | bytes 65568 | tf_op jit(solution)/shard_map/ppermute | solution.py:436
  8.9 1.4 %collective-permute-done.1.high_ref = f32[32,512]{1,0:T(8,128)S(1)} collective-permute-done((f32[32,512]{1,0:T(8,128)S(1)}, f32[32,512]{1,0:T(8,128)S(1)}, u32[]{:S(2)}, u32[]{:S(2)}) %collective-permute-start.1) | collective-permute-done | bytes 65568 | tf_op jit(solution)/shard_map/ppermute | solution.py:437
  10.4 1.2 %correct.1 = f32[8,8,3072]{2,1,0:T(8,128)} custom-call(f32[32,512]{1,0:T(8,128)S(1)} %collective-permute-done.low_ref, f32[32,512]{1,0:T(8,128)S(1)} %collective-permute-done.1.high_ref, f32[8,8,3072]{2,1,0:T(8,128)S(1)} %forecast.1.in_ref), custom_call_target="tpu_custom_call" | custom-call | tf_op jit(solution)/shard_map/correct/pallas_call | solution.py:451
  11.5 4.9 %all-to-all-start = ((f32[8,8,3072]{2,1,0:T(8,128)}), f32[8,8,3072]{2,1,0:T(8,128)S(1)}, u32[]{:S(2)}, u32[]{:S(2)}) async-start(f32[8,8,3072]{2,1,0:T(8,128)} %correct.1), calls=%async_computation | async-start | bytes 1572864 | tf_op jit(solution)/shard_map/all_to_all | solution.py:460
  16.4 3.8 %collective-permute-start.4 = (f32[16,512]{1,0:T(8,128)S(1)}, f32[16,512]{1,0:T(8,128)S(1)}, u32[]{:S(2)}, u32[]{:S(2)}) collective-permute-start(f32[16,512]{1,0:T(8,128)S(1)} %get-tuple-element.16.refs_0_), channel_id=1, source_target_pairs={{0,6},{1,7},{2,0},{3,1},{4,2},{5,3},{6,4},{7,5},{8,14},{9,15},{10,... | collective-permute-start | bytes 98312 | tf_op jit(solution)/shard_map/ppermute | solution.py:439
  20.2 0.0 collective-permute-start.3
  20.2 1.1 %collective-permute-start.2 = (f32[16,512]{1,0:T(8,128)S(1)}, f32[16,512]{1,0:T(8,128)S(1)}, u32[]{:S(2)}, u32[]{:S(2)}) collective-permute-start(f32[16,512]{1,0:T(8,128)S(1)} %get-tuple-element.16.refs_0_), channel_id=1, source_target_pairs={{0,2},{1,3},{2,4},{3,5},{4,6},{5,7},{6,0},{7,1},{8,10},{9,11},{10,... | collective-permute-start | bytes 98312 | tf_op jit(solution)/shard_map/ppermute | solution.py:439
  21.3 9.7 %collective-permute-done.4.refs_3_ = f32[16,512]{1,0:T(8,128)S(1)} collective-permute-done((f32[16,512]{1,0:T(8,128)S(1)}, f32[16,512]{1,0:T(8,128)S(1)}, u32[]{:S(2)}, u32[]{:S(2)}) %collective-permute-start.4) | collective-permute-done | bytes 32800 | tf_op jit(solution)/shard_map/ppermute | solution.py:439
  31.1 9.1 %collective-permute-done.3.refs_2_ = f32[16,512]{1,0:T(8,128)S(1)} collective-permute-done((f32[16,512]{1,0:T(8,128)S(1)}, f32[16,512]{1,0:T(8,128)S(1)}, u32[]{:S(2)}, u32[]{:S(2)}) %collective-permute-start.3) | collective-permute-done | bytes 32800 | tf_op jit(solution)/shard_map/ppermute | solution.py:439
  40.1 0.0 collective-permute-done.2.refs_1_
  40.2 1.9 %collective-permute-start.7 = (f32[64,512]{1,0:T(8,128)S(1)}, f32[64,512]{1,0:T(8,128)S(1)}, u32[]{:S(2)}, u32[]{:S(2)}) collective-permute-start(f32[64,512]{1,0:T(8,128)S(1)} %stack.1.refs_0_), channel_id=1, source_target_pairs={{0,24},{8,0},{16,8},{24,16},{1,25},{9,1},{17,9},{25,17},{2,26},{10... | collective-permute-start | bytes 393224 | tf_op jit(solution)/shard_map/ppermute | solution.py:467
  42.1 1.5 %collective-permute-start.6 = (f32[64,512]{1,0:T(8,128)S(1)}, f32[64,512]{1,0:T(8,128)S(1)}, u32[]{:S(2)}, u32[]{:S(2)}) collective-permute-start(f32[64,512]{1,0:T(8,128)S(1)} %stack.1.refs_0_), channel_id=1, source_target_pairs={{0,16},{8,24},{16,0},{24,8},{1,17},{9,25},{17,1},{25,9},{2,18},{10... | collective-permute-start | bytes 393224 | tf_op jit(solution)/shard_map/ppermute | solution.py:467
  43.6 0.0 collective-permute-start.5
  43.6 2.1 %collective-permute-done.7.refs_3_ = f32[64,512]{1,0:T(8,128)S(1)} collective-permute-done((f32[64,512]{1,0:T(8,128)S(1)}, f32[64,512]{1,0:T(8,128)S(1)}, u32[]{:S(2)}, u32[]{:S(2)}) %collective-permute-start.7) | collective-permute-done | bytes 131104 | tf_op jit(solution)/shard_map/ppermute | solution.py:467
  45.8 4.1 %collective-permute-done.6.refs_2_ = f32[64,512]{1,0:T(8,128)S(1)} collective-permute-done((f32[64,512]{1,0:T(8,128)S(1)}, f32[64,512]{1,0:T(8,128)S(1)}, u32[]{:S(2)}, u32[]{:S(2)}) %collective-permute-start.6) | collective-permute-done | bytes 131104 | tf_op jit(solution)/shard_map/ppermute | solution.py:467
  49.9 0.0 collective-permute-done.5.refs_1_
  49.9 0.1 collective-permute-start.8
  50.0 0.0 copy-done.3
  50.0 0.0 copy-done.1
  50.0 0.0 copy-done.2
  50.0 4.3 %taper.1.taper_ref = f32[4,4,256,256]{3,2,1,0:T(8,128)} custom-call(s32[1]{0:T(128)} %bitcast.6.first_ref, s32[4]{0:T(128)S(1)} %copy-done.3, s32[4,256]{1,0:T(4,128)S(1)} %copy-done.1, s32[4,256]{1,0:T(4,128)S(1)} %copy-done.2), custom_call_target="tpu_custom_call" | custom-call | tf_op jit(solution)/shard_map/taper/pallas_call | solution.py:483
  54.3 0.0 collective-permute-done.8.refs_8_
  54.3 0.0 copy-done
  54.3 0.0 copy-done.4
  54.3 0.0 copy-done.5
  54.3 9.2 %chain.1 = (bf16[4,256,192]{2,1,0:T(8,128)(2,1)S(1)}, bf16[4,128,256]{2,1,0:T(8,128)(2,1)S(1)}) custom-call(s32[1]{0:T(128)} %bitcast.4.refs_0_, s32[4]{0:T(128)S(1)} %copy-done.3, s32[4,256]{1,0:T(4,128)S(1)} %copy-done.1, s32[4,256]{1,0:T(4,128)S(1)} %copy-done.2, f32[4,256]{1,0:T(4,128)S(1)} %copy-done.4, f32[4,256]{1,0:T(4,128)S(1)} %copy-done.5, ...), custom_call_target="tpu_custom_call" | custom-call | tf_op jit(solution)/shard_map/chain/pallas_call | solution.py:508
  63.6 0.0 all-to-all-done
  63.6 6.4 %update.1 = f32[64,3072]{1,0:T(8,128)} custom-call(f32[64,3072]{1,0:T(8,128)S(1)} %bitcast.8, bf16[4,256,192]{2,1,0:T(8,128)(2,1)S(1)} %get-tuple-element.17.y_ref, bf16[4,128,256]{2,1,0:T(8,128)(2,1)S(1)} %get-tuple-element.18.w_ref, f32[4,4,256,256]{3,2,1,0:T(8,128)} %taper.1.taper_ref), custom_call_target="tpu_custom_call" | custom-call | tf_op jit(solution)/shard_map/update/pallas_call | solution.py:512
  (2 shorter events, 0.0 us)
Async XLA Ops:
  0.0 50.0 %copy-start.3 = (s32[4]{0:T(128)S(1)}, s32[4]{0:T(128)}, u32[]{:S(2)}) copy-start(s32[4]{0:T(128)} %owner_ref.3) | copy-start | bytes 52
  0.0 50.0 %copy-start.1 = (s32[4,256]{1,0:T(4,128)S(1)}, s32[4,256]{1,0:T(4,128)}, u32[]{:S(2)}) copy-start(s32[4,256]{1,0:T(4,128)} %offset_ref.3) | copy-start | bytes 12292
  0.0 50.0 %copy-start.2 = (s32[4,256]{1,0:T(4,128)S(1)}, s32[4,256]{1,0:T(4,128)}, u32[]{:S(2)}) copy-start(s32[4,256]{1,0:T(4,128)} %cutoff_ref.1) | copy-start | bytes 12292
  2.6 6.3 %collective-permute-start = (f32[32,512]{1,0:T(8,128)S(1)}, f32[32,512]{1,0:T(8,128)S(1)}, u32[]{:S(2)}, u32[]{:S(2)}) collective-permute-start(f32[32,512]{1,0:T(8,128)S(1)} %get-tuple-element.12), channel_id=1, source_target_pairs={{0,8},{8,16},{16,24},{24,0},{1,9},{9,17},{17,25},{25,1},{2,10},{10... | collective-permute-start | bytes 196616 | tf_op jit(solution)/shard_map/ppermute | solution.py:436
  5.7 4.7 %collective-permute-start.1 = (f32[32,512]{1,0:T(8,128)S(1)}, f32[32,512]{1,0:T(8,128)S(1)}, u32[]{:S(2)}, u32[]{:S(2)}) collective-permute-start(f32[32,512]{1,0:T(8,128)S(1)} %get-tuple-element.13), channel_id=1, source_target_pairs={{0,24},{8,0},{16,8},{24,16},{1,25},{9,1},{17,9},{25,17},{2,26},{10... | collective-permute-start | bytes 196616 | tf_op jit(solution)/shard_map/ppermute | solution.py:437
  7.4 46.9 %copy-start = (f32[4,256,64]{1,2,0:T(8,128)S(1)}, f32[4,256,64]{1,2,0:T(8,128)}, u32[]{:S(2)}) copy-start(f32[4,256,64]{1,2,0:T(8,128)} %param.10) | copy-start | bytes 786436
  7.4 46.9 %copy-start.4 = (f32[4,256]{1,0:T(4,128)S(1)}, f32[4,256]{1,0:T(4,128)}, u32[]{:S(2)}) copy-start(f32[4,256]{1,0:T(4,128)} %refs_4_.1) | copy-start | bytes 12292
  7.4 46.9 %copy-start.5 = (f32[4,256]{1,0:T(4,128)S(1)}, f32[4,256]{1,0:T(4,128)}, u32[]{:S(2)}) copy-start(f32[4,256]{1,0:T(4,128)} %refs_5_.1) | copy-start | bytes 12292
  11.5 52.1 %all-to-all-start = ((f32[8,8,3072]{2,1,0:T(8,128)}), f32[8,8,3072]{2,1,0:T(8,128)S(1)}, u32[]{:S(2)}, u32[]{:S(2)}) async-start(f32[8,8,3072]{2,1,0:T(8,128)} %correct.1), calls=%async_computation | async-start | bytes 1572864 | tf_op jit(solution)/shard_map/all_to_all | solution.py:460
  16.4 14.7 %collective-permute-start.4 = (f32[16,512]{1,0:T(8,128)S(1)}, f32[16,512]{1,0:T(8,128)S(1)}, u32[]{:S(2)}, u32[]{:S(2)}) collective-permute-start(f32[16,512]{1,0:T(8,128)S(1)} %get-tuple-element.16.refs_0_), channel_id=1, source_target_pairs={{0,6},{1,7},{2,0},{3,1},{4,2},{5,3},{6,4},{7,5},{8,14},{9,15},{10,... | collective-permute-start | bytes 98312 | tf_op jit(solution)/shard_map/ppermute | solution.py:439
  20.2 19.9 %collective-permute-start.3 = (f32[16,512]{1,0:T(8,128)S(1)}, f32[16,512]{1,0:T(8,128)S(1)}, u32[]{:S(2)}, u32[]{:S(2)}) collective-permute-start(f32[16,512]{1,0:T(8,128)S(1)} %get-tuple-element.16.refs_0_), channel_id=1, source_target_pairs={{0,4},{1,5},{2,6},{3,7},{4,0},{5,1},{6,2},{7,3},{8,12},{9,13},{10,... | collective-permute-start | bytes 98312 | tf_op jit(solution)/shard_map/ppermute | solution.py:439
  20.2 19.9 %collective-permute-start.2 = (f32[16,512]{1,0:T(8,128)S(1)}, f32[16,512]{1,0:T(8,128)S(1)}, u32[]{:S(2)}, u32[]{:S(2)}) collective-permute-start(f32[16,512]{1,0:T(8,128)S(1)} %get-tuple-element.16.refs_0_), channel_id=1, source_target_pairs={{0,2},{1,3},{2,4},{3,5},{4,6},{5,7},{6,0},{7,1},{8,10},{9,11},{10,... | collective-permute-start | bytes 98312 | tf_op jit(solution)/shard_map/ppermute | solution.py:439
  40.2 5.6 %collective-permute-start.7 = (f32[64,512]{1,0:T(8,128)S(1)}, f32[64,512]{1,0:T(8,128)S(1)}, u32[]{:S(2)}, u32[]{:S(2)}) collective-permute-start(f32[64,512]{1,0:T(8,128)S(1)} %stack.1.refs_0_), channel_id=1, source_target_pairs={{0,24},{8,0},{16,8},{24,16},{1,25},{9,1},{17,9},{25,17},{2,26},{10... | collective-permute-start | bytes 393224 | tf_op jit(solution)/shard_map/ppermute | solution.py:467
  42.1 7.8 %collective-permute-start.6 = (f32[64,512]{1,0:T(8,128)S(1)}, f32[64,512]{1,0:T(8,128)S(1)}, u32[]{:S(2)}, u32[]{:S(2)}) collective-permute-start(f32[64,512]{1,0:T(8,128)S(1)} %stack.1.refs_0_), channel_id=1, source_target_pairs={{0,16},{8,24},{16,0},{24,8},{1,17},{9,25},{17,1},{25,9},{2,18},{10... | collective-permute-start | bytes 393224 | tf_op jit(solution)/shard_map/ppermute | solution.py:467
  43.6 6.3 %collective-permute-start.5 = (f32[64,512]{1,0:T(8,128)S(1)}, f32[64,512]{1,0:T(8,128)S(1)}, u32[]{:S(2)}, u32[]{:S(2)}) collective-permute-start(f32[64,512]{1,0:T(8,128)S(1)} %stack.1.refs_0_), channel_id=1, source_target_pairs={{0,8},{8,16},{16,24},{24,0},{1,9},{9,17},{17,25},{25,1},{2,10},{10... | collective-permute-start | bytes 393224 | tf_op jit(solution)/shard_map/ppermute | solution.py:467
  49.9 4.4 %collective-permute-start.8 = (f32[64,512]{1,0:T(8,128)S(1)}, f32[64,512]{1,0:T(8,128)S(1)}, u32[]{:S(2)}, u32[]{:S(2)}) collective-permute-start(f32[64,512]{1,0:T(8,128)S(1)} %sum.1.refs_7_), channel_id=1, source_target_pairs={{0,1},{1,0},{2,3},{3,2},{4,5},{5,4},{6,7},{7,6},{8,9},{9,8},{10,11... | collective-permute-start | bytes 393224 | tf_op jit(solution)/shard_map/ppermute | solution.py:472
